TPU v7x, 32 devices: a whole 2x2x4 slice. The times are simulated.
32 devices in a mesh: dp: 8 (over z, x), seq: 4 (over y, core).
Axes of the slice: x: 2, y: 2, z: 4, core: 2. Of those that a mesh axis runs over, the one named last changes fastest.
Arguments:
- inputs: bfloat16 [16, 2048, 768], P('dp', 'seq'), may hold values from -6 to 6
- lengths: int32 [16], P('dp'), may hold values from 256 to 2048
- first_gain: float32 [768], replicated, may hold values from 0.5 to 1.5
- first_shift: float32 [768], replicated, may hold values from -2 to 2
- query_weight: bfloat16 [768, 768], replicated, may hold values from -0.21875 to 0.21875
- query_bias: float32 [768], replicated, may hold values from -1.5 to 1.5
- key_weight: bfloat16 [768, 768], replicated, may hold values from -0.21875 to 0.21875
- value_weight: bfloat16 [768, 768], replicated, may hold values from -0.21875 to 0.21875
- value_bias: float32 [768], replicated, may hold values from -0.25 to 0.25
- output_weight: bfloat16 [768, 768], replicated, may hold values from -4 to 4
- output_bias: float32 [768], replicated, may hold values from -2 to 2
- second_gain: float32 [768], replicated, may hold values from 0.5 to 1.5
- second_shift: float32 [768], replicated, may hold values from -2 to 2
- inner_weight: bfloat16 [768, 3072], replicated, may hold values from -0.21875 to 0.21875
- inner_bias: float32 [3072], replicated, may hold values from -2 to 2
- outer_weight: bfloat16 [3072, 768], replicated, may hold values from -0.109375 to 0.109375
- outer_bias: float32 [768], replicated, may hold values from -2 to 2
- cotangent: bfloat16 [16, 2048, 768], P('dp', 'seq'), may hold values from -6 to 6
Outputs:
- result: bfloat16 [16, 2048, 768], P('dp', 'seq')
- grad_inputs: bfloat16 [16, 2048, 768], P('dp', 'seq')
- grad_first_gain: float32 [768], replicated
- grad_first_shift: float32 [768], replicated
- grad_query_weight: float32 [768, 768], P('dp')
- grad_query_bias: float32 [768], replicated
- grad_key_weight: float32 [768, 768], P('dp')
- grad_value_weight: float32 [768, 768], P('dp')
- grad_value_bias: float32 [768], replicated
- grad_output_weight: float32 [768, 768], P('dp')
- grad_output_bias: float32 [768], replicated
- grad_second_gain: float32 [768], replicated
- grad_second_shift: float32 [768], replicated
- grad_inner_weight: float32 [768, 3072], P('dp')
- grad_inner_bias: float32 [3072], replicated
- grad_outer_weight: float32 [3072, 768], P('dp')
- grad_outer_bias: float32 [768], replicated
- stream_scale: float32 [], replicated
- attention_scale: float32 [], replicated
- feedforward_scale: float32 [], replicated
All inputs are finite; a program needn't handle non-finite values.
Results may differ from a plain program's by a relative error of at most 0.012.
Values may be sent and summed in bfloat16 or wider, within the bound.
A program may use at most 256 MiB of HBM per device.

v0:
```python
import functools

import jax
import jax.numpy as jnp
from jax import lax
from jax.experimental import pallas as pl
from jax.experimental.pallas import tpu as pltpu
from jax.sharding import PartitionSpec as P

HEADS = 12
HEAD_DIM = 64
EPSILON = 1e-12
NEGATIVE = -1e30
PAIR = 2 * HEAD_DIM
NT = ((1,), (1,))
NN = ((1,), (0,))
TN = ((0,), (0,))


def norm_apply(values, gain_vec, shift_vec):
    average = jnp.mean(values, axis=-1, keepdims=True)
    centered = values - average
    spread = jnp.mean(centered * centered, axis=-1, keepdims=True)
    return centered * lax.rsqrt(spread + EPSILON) * gain_vec + shift_vec


def dot(left, right, dims):
    return lax.dot_general(left, right, (dims, ((), ())), preferred_element_type=jnp.float32)


def block_places():
    seq = lax.axis_index("seq")
    beside = seq + 1 - 2 * lax.rem(seq, 2)
    return seq, lax.rem(seq + 2, 4), beside, lax.rem(beside + 2, 4)


def own_length(lengths_ref):
    return lengths_ref[lax.axis_index("seq") // 2]


def key_valid(lengths_ref, keys_total):
    block = keys_total // 4
    spots = lax.broadcasted_iota(jnp.int32, (keys_total, 1), 0)
    shift = 0
    for index, place in enumerate(block_places()):
        shift = jnp.where(spots >= index * block, (place - index) * block, shift)
    return spots + shift < own_length(lengths_ref)


def attend_body(
    info_ref, q_ref, k_ref, v_ref, cot_ref, out_ref, lse_ref, far_ref, swap_sems
):
    bits, across = where_am_i()
    swap = swap_copy(cot_ref.at[1 - bits["y"]], far_ref, swap_sems, across)
    now = pl.program_id(0) * pl.num_programs(1) + pl.program_id(1)

    @pl.when(now == 0)
    def _():
        greet(across, ("y",))
        swap.start()

    lane = lax.broadcasted_iota(jnp.int32, (1, PAIR), 1)
    scale = jnp.bfloat16(HEAD_DIM ** (-0.5))
    queries = q_ref[...] * scale
    keys = k_ref[...]
    values_t = v_ref[...].T
    valid = key_valid(info_ref, keys.shape[0])
    outs = []
    for head in range(2):
        mine = (lane < HEAD_DIM) if head == 0 else (lane >= HEAD_DIM)
        scores = dot(keys, jnp.where(mine, queries, jnp.zeros_like(queries)), NT)
        scores = jnp.where(valid, scores, NEGATIVE)
        top = jnp.max(scores, axis=0, keepdims=True)
        weights = jnp.exp(scores - top)
        total = jnp.sum(weights, axis=0, keepdims=True)
        mixed = dot(
            values_t[HEAD_DIM * head : HEAD_DIM * (head + 1)], weights.astype(jnp.bfloat16), NN
        )
        outs.append(mixed * (1.0 / total))
        lse_ref[0, head : head + 1, :] = top + jnp.log(total)
    out_ref[...] = jnp.concatenate(outs, axis=0).T.astype(jnp.bfloat16)

    @pl.when(now == pl.num_programs(0) * pl.num_programs(1) - 1)
    def _():
        swap.wait()


def attend(info, queries, keys, values, cotangent, block, collective):
    tokens, width = queries.shape
    total = keys.shape[0]
    pairs = width // PAIR
    q_spec = pl.BlockSpec((block, PAIR), lambda h, i, n: (i, h))
    k_spec = pl.BlockSpec((total, PAIR), lambda h, i, n: (0, h))
    return pl.pallas_call(
        attend_body,
        grid_spec=pltpu.PrefetchScalarGridSpec(
            num_scalar_prefetch=1,
            grid=(pairs, tokens // block),
            in_specs=[q_spec, k_spec, k_spec, pl.BlockSpec(memory_space=pl.ANY)],
            out_specs=[
                q_spec,
                pl.BlockSpec((1, 2, block), lambda h, i, n: (h, 0, i)),
                pl.BlockSpec(memory_space=pl.ANY),
            ],
            scratch_shapes=[pltpu.SemaphoreType.DMA((2,))],
        ),
        out_shape=[
            jax.ShapeDtypeStruct((tokens, width), jnp.bfloat16),
            jax.ShapeDtypeStruct((pairs, 2, tokens), jnp.float32),
            jax.ShapeDtypeStruct(cotangent.shape[1:], cotangent.dtype),
        ],
        compiler_params=pltpu.CompilerParams(
            collective_id=collective, has_side_effects=True, vmem_limit_bytes=48 << 20
        ),
        cost_estimate=pl.CostEstimate(
            flops=16 * tokens * total * width, bytes_accessed=1 << 23, transcendentals=0
        ),
        name="attend",
    )(info, queries, keys, values, cotangent)


def attend_back_body(
    info_ref,
    q_ref,
    k_ref,
    v_ref,
    do_ref,
    o_ref,
    lse_ref,
    dq_ref,
    dk_ref,
    dv_ref,
    dk_acc,
    dv_acc,
    before=None,
    after=None,
):
    step = pl.program_id(1)
    lane = lax.broadcasted_iota(jnp.int32, (1, PAIR), 1)
    scale = jnp.bfloat16(HEAD_DIM ** (-0.5))
    grad_out = do_ref[...]
    queries = q_ref[...] * scale
    keys = k_ref[...]
    keys_t = keys.T
    values = v_ref[...]
    product = grad_out.astype(jnp.float32) * o_ref[...].astype(jnp.float32)
    pick = (
        lax.broadcasted_iota(jnp.int32, (8, PAIR), 1) // HEAD_DIM
        == lax.broadcasted_iota(jnp.int32, (8, PAIR), 0)
    ).astype(jnp.float32)
    row_sums = lax.dot_general(
        pick,
        product,
        (NT, ((), ())),
        precision=lax.Precision.HIGHEST,
        preferred_element_type=jnp.float32,
    )
    valid = key_valid(info_ref, keys.shape[0])
    zero = jnp.zeros_like(queries)
    grad_k = 0
    grad_v = 0
    grad_q = []
    for head in range(2):
        if before is not None:
            before(head)
        mine = (lane < HEAD_DIM) if head == 0 else (lane >= HEAD_DIM)
        query_h = jnp.where(mine, queries, zero)
        out_h = jnp.where(mine, grad_out, zero)
        scores = jnp.where(valid, dot(keys, query_h, NT), NEGATIVE)
        weights = jnp.exp(scores - lse_ref[0, head : head + 1, :])
        grad_w = dot(values, out_h, NT)
        grad_s = (weights * (grad_w - row_sums[head : head + 1])).astype(jnp.bfloat16)
        grad_v = grad_v + dot(weights.astype(jnp.bfloat16), out_h, NN)
        grad_k = grad_k + dot(grad_s, query_h, NN)
        grad_q.append(dot(keys_t[HEAD_DIM * head : HEAD_DIM * (head + 1)], grad_s, NN))
    grad_q = jnp.concatenate(grad_q, axis=0) * (HEAD_DIM ** (-0.5))
    dq_ref[...] = grad_q.T.astype(jnp.bfloat16)

    @pl.when(step == 0)
    def _():
        dk_acc[...] = grad_k
        dv_acc[...] = grad_v

    @pl.when(step > 0)
    def _():
        dk_acc[...] += grad_k
        dv_acc[...] += grad_v

    @pl.when(step == pl.num_programs(1) - 1)
    def _():
        near = dk_ref.shape[0]
        dk_ref[...] = dk_acc[:near].astype(jnp.bfloat16)
        dv_ref[...] = dv_acc[:near].astype(jnp.bfloat16)
        if after is not None:
            after()


def attend_back(info, queries, keys, values, grad_out, out, log_sums, block):
    tokens, width = queries.shape
    total = keys.shape[0]
    pairs = width // PAIR
    q_spec = pl.BlockSpec((block, PAIR), lambda h, i, n: (i, h))
    k_spec = pl.BlockSpec((total, PAIR), lambda h, i, n: (0, h))
    return pl.pallas_call(
        attend_back_body,
        grid_spec=pltpu.PrefetchScalarGridSpec(
            num_scalar_prefetch=1,
            grid=(pairs, tokens // block),
            in_specs=[
                q_spec,
                k_spec,
                k_spec,
                q_spec,
                q_spec,
                pl.BlockSpec((1, 2, block), lambda h, i, n: (h, 0, i)),
            ],
            out_specs=[q_spec, k_spec, k_spec],
            scratch_shapes=[pltpu.VMEM((total, PAIR), jnp.float32)] * 2,
        ),
        out_shape=[
            jax.ShapeDtypeStruct((tokens, width), jnp.bfloat16),
            jax.ShapeDtypeStruct((total, width), jnp.bfloat16),
            jax.ShapeDtypeStruct((total, width), jnp.bfloat16),
        ],
        compiler_params=pltpu.CompilerParams(vmem_limit_bytes=48 << 20),
        cost_estimate=pl.CostEstimate(
            flops=40 * tokens * total * width, bytes_accessed=1 << 24, transcendentals=0
        ),
        name="attend_back",
    )(info, queries, keys, values, grad_out, out, log_sums)


MESH_IDS = pl.DeviceIdType.MESH
AXES = ("zhi", "zlo", "x", "y")
LATE = (("x", "zlo", "y", "zhi"), ("zlo", "x", "y", "zhi"), ("x", "zlo", "zhi", "y"))


def where_am_i():
    data = lax.axis_index("dp")
    seq = lax.axis_index("seq")
    bits = {
        "zhi": data // 4,
        "zlo": (data // 2) % 2,
        "x": data % 2,
        "y": seq // 2,
        "core": seq % 2,
    }

    def across(axis):
        if axis == "core":
            return (data, seq + 1 - 2 * bits["core"])
        if axis == "y":
            return (data, seq + 2 - 4 * bits["y"])
        step = {"zhi": 4, "zlo": 2, "x": 1}[axis]
        return (data + step - 2 * step * bits[axis], seq)

    return bits, across


def spot_of(piece, order):
    bits = {axis: (piece >> (3 - k)) & 1 for k, axis in enumerate(AXES)}
    return sum(bits[axis] << (3 - k) for k, axis in enumerate(order))


class Color:
    def __init__(self, source, acc, lands, gathers, sems, order):
        self.source, self.acc, self.lands, self.gathers = source, acc, lands, gathers
        self.sems, self.order = sems, order
        self.pieces, self.rows, self.cols = acc.shape
        self.bits, self.across = where_am_i()

    def base(self, stage):
        return sum(self.bits[self.order[k]] * (self.pieces >> (k + 1)) for k in range(stage))

    def remote(self, src, dst, slot, axis):
        return pltpu.make_async_remote_copy(
            src_ref=src,
            dst_ref=dst,
            send_sem=self.sems.at[0, slot],
            recv_sem=self.sems.at[1, slot],
            device_id=self.across(axis),
            device_id_type=MESH_IDS,
        )

    def begin(self):
        core = self.bits["core"]
        mine = pl.ds(pl.multiple_of(core * self.cols, 128), self.cols)
        theirs = pl.ds(pl.multiple_of((1 - core) * self.cols, 128), self.cols)
        for piece in range(self.pieces):
            spot = spot_of(piece, self.order)
            span = pl.ds(piece * self.rows, self.rows)
            self.remote(
                self.source.at[span, theirs], self.lands[0].at[spot], 0, "core"
            ).start()
            pltpu.make_async_copy(
                self.source.at[span, mine], self.acc.at[spot], self.sems.at[0, 7]
            ).start()

    def add(self, base, count, land):
        @pl.loop(0, count)
        def _(index):
            total = self.acc[base + index].astype(jnp.float32) + land[index].astype(jnp.float32)
            self.acc[base + index] = total.astype(jnp.bfloat16)

    def transfer(self, stage):
        if stage < 4:
            axis = self.order[stage]
            half = self.pieces >> (stage + 1)
            start = self.base(stage) + (1 - self.bits[axis]) * half
            return self.remote(
                self.acc.at[pl.ds(start, half)], self.lands[stage + 1], stage + 1, axis
            )
        if stage == 4:
            there = self.gathers[0].at[self.bits["y"]]
            return self.remote(self.acc.at[self.base(4)], there, 5, "y")
        return self.remote(self.gathers[0], self.gathers[1], 6, "core")

    def step(self, stage):
        if stage == 0:
            whole = self.remote(self.lands[0], self.lands[0], 0, "core")
            pltpu.make_async_copy(self.acc, self.acc, self.sems.at[0, 7]).wait()
            whole.wait_send()
            whole.wait_recv()
        else:
            self.transfer(stage - 1).wait()
        if stage <= 4:
            self.add(self.base(stage), self.pieces >> stage, self.lands[stage])
        if stage == 4:
            self.gathers[0][self.bits["y"]] = self.acc[self.base(4)]
        if stage < 6:
            self.transfer(stage).start()


def swap_copy(source, landing, sems, across):
    return pltpu.make_async_remote_copy(
        src_ref=source,
        dst_ref=landing,
        send_sem=sems.at[0],
        recv_sem=sems.at[1],
        device_id=across("y"),
        device_id_type=MESH_IDS,
    )


def greet(across, axes=("core", *AXES)):
    barrier = pltpu.get_barrier_semaphore()
    for axis in axes:
        pl.semaphore_signal(barrier, inc=1, device_id=across(axis), device_id_type=MESH_IDS)
    pl.semaphore_wait(barrier, len(axes))


CHUNKS = 4


def enter_body(
    in_ref,
    gain_ref,
    shift_ref,
    q_bias_ref,
    v_bias_ref,
    wq_ref,
    wk_ref,
    wv_ref,
    x_ref,
    normed_ref,
    q_ref,
    k_ref,
    v_ref,
    swap_sems,
    own_sem,
    trade_sems,
):
    low = jnp.bfloat16
    bits, across = where_am_i()
    row = bits["y"]
    size = x_ref.shape[0] // CHUNKS
    tokens = x_ref.shape[0]
    half = CHUNKS // 2
    own = pltpu.make_async_copy(in_ref.at[row], x_ref.at[pl.ds(0, tokens // 2)], own_sem)
    own.start()
    greet(across, ("core", "y"))

    def arrival(chunk):
        return pltpu.make_async_remote_copy(
            src_ref=in_ref.at[1 - row, pl.ds(pl.multiple_of(chunk * size, size), size)],
            dst_ref=x_ref.at[pl.ds(pl.multiple_of((half + chunk) * size, size), size)],
            send_sem=swap_sems.at[0, chunk],
            recv_sem=swap_sems.at[1, chunk],
            device_id=across("y"),
            device_id_type=MESH_IDS,
        )

    def trade(chunk, which):
        ref = (k_ref, v_ref)[which]
        return pltpu.make_async_remote_copy(
            src_ref=ref.at[pl.ds(pl.multiple_of(chunk * size, size), size)],
            dst_ref=ref.at[pl.ds(pl.multiple_of(tokens + chunk * size, size), size)],
            send_sem=trade_sems.at[0, which, chunk],
            recv_sem=trade_sems.at[1, which, chunk],
            device_id=across("core"),
            device_id_type=MESH_IDS,
        )

    for chunk in range(half):
        arrival(chunk).start()
    own.wait()

    @pl.loop(0, CHUNKS)
    def _(chunk):
        @pl.when(chunk >= half)
        def _():
            arrival(chunk - half).wait()

        span = pl.ds(pl.multiple_of(chunk * size, size), size)
        rows = x_ref[span, :].astype(jnp.float32)
        normed = norm_apply(rows, gain_ref[...], shift_ref[...]).astype(low)
        normed_ref[span, :] = normed
        k_ref[span, :] = dot(normed, wk_ref[...], NN).astype(low)
        trade(chunk, 0).start()
        v_ref[span, :] = (dot(normed, wv_ref[...], NN) + v_bias_ref[...]).astype(low)
        trade(chunk, 1).start()
        q_ref[span, :] = (dot(normed, wq_ref[...], NN) + q_bias_ref[...]).astype(low)

    @pl.loop(0, CHUNKS)
    def _(chunk):
        trade(chunk, 0).wait()
        trade(chunk, 1).wait()


def enter(inputs, gain, shift, q_bias, v_bias, wq, wk, wv, collective):
    _, local_len, width = inputs.shape
    vmem = pl.BlockSpec(memory_space=pltpu.VMEM)

    def made(blocks):
        return jax.ShapeDtypeStruct((blocks * local_len, width), jnp.bfloat16)

    return pl.pallas_call(
        enter_body,
        out_shape=[made(2), made(2), made(2), made(4), made(4)],
        in_specs=[pl.BlockSpec(memory_space=pl.ANY)] + [vmem] * 7,
        out_specs=[vmem] * 5,
        scratch_shapes=[
            pltpu.SemaphoreType.DMA((2, CHUNKS // 2)),
            pltpu.SemaphoreType.DMA,
            pltpu.SemaphoreType.DMA((2, 2, CHUNKS)),
        ],
        compiler_params=pltpu.CompilerParams(
            collective_id=collective, has_side_effects=True, vmem_limit_bytes=48 << 20
        ),
        name="enter",
    )(inputs, gain[None], shift[None], q_bias[None], v_bias[None], wq, wk, wv)


def color_scratch(arrays):
    scratch = []
    outs = []
    for array in arrays:
        rows, cols = array.shape[0] // 16, array.shape[1] // 2
        scratch.append(pltpu.VMEM((16, rows, cols), jnp.bfloat16))
        for size in (16, 8, 4, 2, 1):
            scratch.append(pltpu.VMEM((size, rows, cols), jnp.bfloat16))
        scratch += [pltpu.VMEM((2, rows, cols), jnp.bfloat16)] * 2
        scratch.append(pltpu.SemaphoreType.DMA((2, 8)))
        outs += [jax.ShapeDtypeStruct((2, rows, cols), jnp.bfloat16)] * 2
    return scratch, outs


def colors_of(sources, scratch, orders):
    colors = []
    for index, source in enumerate(sources):
        acc, *lands = scratch[9 * index : 9 * index + 6]
        gathers = scratch[9 * index + 6 : 9 * index + 8]
        sems = scratch[9 * index + 8]
        colors.append(Color(source, acc, lands, gathers, sems, orders[index]))
    return colors


def hand_out(colors, outs):
    for index, color in enumerate(colors):
        outs[2 * index][...] = color.gathers[0][...]
        outs[2 * index + 1][...] = color.gathers[1][...]


def assemble(arrays, got):
    core = lax.axis_index("seq") % 2
    sums = []
    for index, array in enumerate(arrays):
        mine, other = got[2 * index], got[2 * index + 1]
        rows = array.shape[0] // 8
        left = jnp.where(core == 0, mine, other).reshape(rows, -1)
        right = jnp.where(core == 0, other, mine).reshape(rows, -1)
        sums.append(jnp.concatenate([left, right], axis=1).astype(jnp.float32))
    return sums


def vector_sum(source, held, lands, sems, bits_across):
    bits, across = bits_across
    held[...] = source[...]
    for slot, axis in enumerate(("core", "y", "x", "zlo", "zhi")):
        copy = pltpu.make_async_remote_copy(
            src_ref=held,
            dst_ref=lands.at[slot],
            send_sem=sems.at[0, slot],
            recv_sem=sems.at[1, slot],
            device_id=across(axis),
            device_id_type=MESH_IDS,
        )
        copy.start()
        yield
        copy.wait()
        held[...] = held[...] + lands[slot]


def reduce_body(count, orders, *refs):
    sources, vector, far = refs[:count], refs[count], refs[count + 1]
    outs = refs[count + 2 : count + 2 + 2 * count]
    vector_out, far_out = refs[3 * count + 2 : 3 * count + 4]
    swap_sems, *scratch = refs[3 * count + 4 :]
    bits, across = where_am_i()
    greet(across)
    swap = swap_copy(far, far_out, swap_sems, across)
    swap.start()
    colors = colors_of(sources, scratch, orders)
    vector_lands, vector_sems = scratch[9 * count :]
    small = vector_sum(vector, vector_out, vector_lands, vector_sems, (bits, across))
    for color in colors:
        color.begin()
    next(small)
    for stage in range(7):
        for color in colors:
            color.step(stage)
        next(small, None)
    hand_out(colors, outs)
    swap.wait()


def reduce_all(arrays, orders, vector, far, collective):
    scratch, outs = color_scratch(arrays)
    scratch.append(pltpu.VMEM((5, *vector.shape), jnp.float32))
    scratch.append(pltpu.SemaphoreType.DMA((2, 5)))
    outs.append(jax.ShapeDtypeStruct(vector.shape, jnp.float32))
    outs.append(jax.ShapeDtypeStruct(far.shape, far.dtype))
    anywhere = pl.BlockSpec(memory_space=pl.ANY)
    vmem = pl.BlockSpec(memory_space=pltpu.VMEM)
    got = pl.pallas_call(
        functools.partial(reduce_body, len(arrays), orders),
        out_shape=outs,
        in_specs=[*[anywhere] * len(arrays), vmem, anywhere],
        out_specs=[*[vmem] * (len(outs) - 1), anywhere],
        scratch_shapes=[pltpu.SemaphoreType.DMA((2,)), *scratch],
        compiler_params=pltpu.CompilerParams(
            collective_id=collective, has_side_effects=True, vmem_limit_bytes=40 << 20
        ),
        cost_estimate=pl.CostEstimate(flops=1 << 34, bytes_accessed=1 << 24, transcendentals=0),
        name="reduce_all",
    )(*arrays, vector, far)
    return assemble(arrays, got), got[-2], got[-1]


TIMES = ((3, 11, 15, 17, 20, 22, 24), (4, 12, 16, 18, 21, 22, 24), (5, 8, 10, 13, 16, 19, 21))
EARLY = (("x", "y", "zlo", "zhi"), ("zlo", "x", "y", "zhi"), ("y", "x", "zlo", "zhi"))


def attend_back_reduce_body(count, orders, *refs):
    info_ref, *blocks = refs[:7]
    swap_in, *sources = refs[7 : 8 + count]
    results = refs[8 + count : 11 + count]
    outs = refs[11 + count : 11 + 3 * count]
    far = refs[11 + 3 * count : 13 + 3 * count]
    swap_out = refs[13 + 3 * count]
    dk_acc, dv_acc, send_k, send_v, trade_sems, swap_sems, *scratch = refs[14 + 3 * count :]
    pair = pl.program_id(0)
    pairs = pl.num_programs(0)
    now = 2 * (pair * pl.num_programs(1) + pl.program_id(1))
    last = 2 * pairs * pl.num_programs(1)
    bits, across = where_am_i()
    colors = colors_of(sources, scratch, orders)

    def trade(index, which):
        return pltpu.make_async_remote_copy(
            src_ref=(send_k, send_v)[which].at[index],
            dst_ref=far[which].at[:, pl.ds(pl.multiple_of(index * PAIR, PAIR), PAIR)],
            send_sem=trade_sems.at[0, which, index],
            recv_sem=trade_sems.at[1, which, index],
            device_id=across("core"),
            device_id_type=MESH_IDS,
        )

    def before(head):
        if head == 0:

            @pl.when(now == 0)
            def _():
                greet(across)
                swap_copy(swap_in, swap_out, swap_sems, across).start()
                for color in colors:
                    color.begin()

        for when in sorted({when for times in TIMES for when in times if when % 2 == head}):

            @pl.when(now + head == when)
            def _(when=when):
                for color, times in zip(colors, TIMES):
                    for stage in range(7):
                        if times[stage] == when:
                            color.step(stage)

    def after():
        near = results[1].shape[0]
        send_k[pair] = dk_acc[near:].astype(jnp.bfloat16)
        send_v[pair] = dv_acc[near:].astype(jnp.bfloat16)
        trade(pair, 0).start()
        trade(pair, 1).start()

    attend_back_body(info_ref, *blocks, *results, dk_acc, dv_acc, before, after)

    @pl.when(now + 2 == last)
    def _():
        for color, times in zip(colors, TIMES):
            for stage in range(7):
                if times[stage] >= last:
                    color.step(stage)
        hand_out(colors, outs)
        swap_copy(swap_in, swap_out, swap_sems, across).wait()

        @pl.loop(0, pairs)
        def _(index):
            trade(index, 0).wait()
            trade(index, 1).wait()


def attend_back_reduce(
    info, queries, keys, values, grad_out, out, log_sums, block, swap, arrays, orders, collective
):
    tokens, width = queries.shape
    total = keys.shape[0]
    near = total // 2
    pairs = width // PAIR
    scratch, outs = color_scratch(arrays)
    q_spec = pl.BlockSpec((block, PAIR), lambda h, i, n: (i, h))
    k_spec = pl.BlockSpec((total, PAIR), lambda h, i, n: (0, h))
    near_spec = pl.BlockSpec((near, PAIR), lambda h, i, n: (0, h))
    whole = pl.BlockSpec(memory_space=pltpu.VMEM)
    anywhere = pl.BlockSpec(memory_space=pl.ANY)
    far = jax.ShapeDtypeStruct((near, width), jnp.bfloat16)
    got = pl.pallas_call(
        functools.partial(attend_back_reduce_body, len(arrays), orders),
        grid_spec=pltpu.PrefetchScalarGridSpec(
            num_scalar_prefetch=1,
            grid=(pairs, tokens // block),
            in_specs=[
                q_spec,
                k_spec,
                k_spec,
                q_spec,
                q_spec,
                pl.BlockSpec((1, 2, block), lambda h, i, n: (h, 0, i)),
                *[anywhere] * (1 + len(arrays)),
            ],
            out_specs=[q_spec, near_spec, near_spec, *[whole] * len(outs), *[anywhere] * 3],
            scratch_shapes=[
                pltpu.VMEM((total, PAIR), jnp.float32),
                pltpu.VMEM((total, PAIR), jnp.float32),
                pltpu.VMEM((pairs, near, PAIR), jnp.bfloat16),
                pltpu.VMEM((pairs, near, PAIR), jnp.bfloat16),
                pltpu.SemaphoreType.DMA((2, 2, pairs)),
                pltpu.SemaphoreType.DMA((2,)),
                *scratch,
            ],
        ),
        out_shape=[
            jax.ShapeDtypeStruct((tokens, width), jnp.bfloat16),
            jax.ShapeDtypeStruct((near, width), jnp.bfloat16),
            jax.ShapeDtypeStruct((near, width), jnp.bfloat16),
            *outs,
            far,
            far,
            jax.ShapeDtypeStruct(swap.shape, swap.dtype),
        ],
        compiler_params=pltpu.CompilerParams(
            collective_id=collective, has_side_effects=True, vmem_limit_bytes=62 << 20
        ),
        cost_estimate=pl.CostEstimate(
            flops=40 * tokens * total * width, bytes_accessed=1 << 25, transcendentals=0
        ),
        name="attend_back_reduce",
    )(info, queries, keys, values, grad_out, out, log_sums, swap, *arrays)

    def joined(own, other):
        return (own.astype(jnp.float32) + other.astype(jnp.float32)).astype(jnp.bfloat16)

    grads = (got[0], joined(got[1], got[-3]), joined(got[2], got[-2]))
    return grads, got[-1], assemble(arrays, got[3:-3])


def feed_body(
    lengths_ref,
    x_ref,
    att_ref,
    cot_ref,
    cot_far_ref,
    gain_ref,
    shift_ref,
    out_bias_ref,
    outer_bias_ref,
    inner_bias_ref,
    wo_ref,
    wi_ref,
    wf_ref,
    result_ref,
    normed_ref,
    act_ref,
    g_inner_ref,
    g_ffn_ref,
    g_attn_ref,
    g_att_ref,
    g_hidden_ref,
    sums_ref,
):
    low = jnp.bfloat16
    width = x_ref.shape[1]
    inner_total = inner_bias_ref.shape[1]
    gain, shift = gain_ref[...], shift_ref[...]
    out_bias, outer_bias = out_bias_ref[...], outer_bias_ref[...]
    own = pl.program_id(0) == 0
    block = x_ref.shape[0]
    seq = lax.axis_index("seq")
    start_at = jnp.where(own, seq, lax.rem(seq + 2, 4)) * block
    spots = lax.broadcasted_iota(jnp.int32, (block, 1), 0) + start_at
    keep = (spots < own_length(lengths_ref)).astype(jnp.float32)
    cot = jnp.where(own, cot_ref[...], cot_far_ref[...])
    branch_attn = dot(att_ref[...], wo_ref[...], NN) + out_bias
    hidden = x_ref[...].astype(jnp.float32) + branch_attn
    centered = hidden - jnp.mean(hidden, axis=-1, keepdims=True)
    spread = lax.rsqrt(jnp.mean(centered * centered, axis=-1, keepdims=True) + EPSILON)
    normal = centered * spread
    normed = (normal * gain + shift).astype(low)
    normed_ref[...] = normed
    g_stream = keep * cot.astype(jnp.float32)
    g_ffn = g_stream.astype(low)
    g_ffn_ref[...] = g_ffn
    branch = jnp.zeros_like(hidden) + outer_bias
    g_normed = jnp.zeros_like(hidden)
    sums = []
    for start in range(0, inner_total, width):
        span = slice(start, start + width)
        inner = dot(normed, wi_ref[:, span], NN) + inner_bias_ref[:, span]
        g_act = dot(g_ffn, wf_ref[span, :], NT)
        cdf = 0.5 + 0.5 * lax.erf(inner * (0.5**0.5))
        act = (inner * cdf).astype(low)
        slope = cdf + inner * (jnp.exp(-0.5 * inner * inner) * ((0.5 / jnp.pi) ** 0.5))
        g_inner = (g_act * slope).astype(low)
        act_ref[:, span] = act
        g_inner_ref[:, span] = g_inner
        branch = branch + dot(act, wf_ref[span, :], NN)
        g_normed = g_normed + dot(g_inner, wi_ref[:, span], NT)
        sums.append(jnp.sum(g_inner.astype(jnp.float32), axis=0, keepdims=True))
    stream = keep * (hidden + branch)
    result_ref[...] = stream.astype(low)
    e = g_normed * gain
    g_hidden = g_stream + spread * (
        e
        - jnp.mean(e, axis=-1, keepdims=True)
        - normal * jnp.mean(e * normal, axis=-1, keepdims=True)
    )
    g_hidden_ref[...] = g_hidden
    g_attn = g_hidden.astype(low)
    g_attn_ref[...] = g_attn
    g_att_ref[...] = dot(g_attn, wo_ref[...], NT).astype(low)
    for item in (
        stream * stream,
        keep * branch_attn * branch_attn,
        keep * branch * branch,
        jnp.broadcast_to(keep, hidden.shape),
        g_attn.astype(jnp.float32),
        g_normed * normal,
        g_normed,
        g_ffn.astype(jnp.float32),
    ):
        sums.append(jnp.sum(item, axis=0, keepdims=True))
    block = jnp.concatenate(sums, axis=0)

    @pl.when(pl.program_id(0) == 0)
    def _():
        sums_ref[...] = block

    @pl.when(pl.program_id(0) > 0)
    def _():
        sums_ref[...] += block


def feed(lengths, x, att, cot, cot_far, vectors, wo, wi, wf):
    tokens, width = x.shape
    inner_total = wi.shape[1]
    low = jnp.bfloat16
    block = tokens // 2
    slot = pl.BlockSpec((block, width), lambda i, n: (i, 0))
    wide = pl.BlockSpec((block, inner_total), lambda i, n: (i, 0))

    def fixed(shape):
        return pl.BlockSpec(shape, lambda i, n: (0, 0), pipeline_mode=pl.Buffered(1))

    sums_rows = inner_total // width + 8
    return pl.pallas_call(
        feed_body,
        grid_spec=pltpu.PrefetchScalarGridSpec(
            num_scalar_prefetch=1,
            grid=(2,),
            in_specs=[
                slot,
                slot,
                fixed(cot.shape),
                fixed(cot.shape),
                *[fixed((1, item.shape[0])) for item in vectors],
                fixed(wo.shape),
                fixed(wi.shape),
                fixed(wf.shape),
            ],
            out_specs=[
                slot,
                slot,
                wide,
                wide,
                slot,
                slot,
                slot,
                slot,
                pl.BlockSpec((sums_rows, width), lambda i, n: (0, 0)),
            ],
        ),
        out_shape=[
            jax.ShapeDtypeStruct((tokens, width), low),
            jax.ShapeDtypeStruct((tokens, width), low),
            jax.ShapeDtypeStruct((tokens, inner_total), low),
            jax.ShapeDtypeStruct((tokens, inner_total), low),
            jax.ShapeDtypeStruct((tokens, width), low),
            jax.ShapeDtypeStruct((tokens, width), low),
            jax.ShapeDtypeStruct((tokens, width), low),
            jax.ShapeDtypeStruct((tokens, width), jnp.float32),
            jax.ShapeDtypeStruct((sums_rows, width), jnp.float32),
        ],
        compiler_params=pltpu.CompilerParams(vmem_limit_bytes=60 << 20),
        cost_estimate=pl.CostEstimate(
            flops=4 * tokens * width * (width + 2 * inner_total),
            bytes_accessed=1 << 25,
            transcendentals=0,
        ),
        name="feed",
    )(lengths, x, att, cot, cot_far, *[item[None] for item in vectors], wo, wi, wf)


def local(
    inputs,
    lengths,
    first_gain,
    first_shift,
    query_weight,
    query_bias,
    key_weight,
    value_weight,
    value_bias,
    output_weight,
    output_bias,
    second_gain,
    second_shift,
    inner_weight,
    inner_bias,
    outer_weight,
    outer_bias,
    cotangent,
):
    groups = lax.axis_size("seq")
    seq_count, local_len, width = inputs.shape
    full_len = local_len * groups
    tokens_here = seq_count * local_len
    place = lax.axis_index("seq")
    half = groups // 2
    row = place // half
    across = [(i, (i + half) % groups) for i in range(groups)]
    beside = [(i, i ^ 1) for i in range(groups)]

    def mine_of(array):
        return lax.dynamic_index_in_dim(array, row, 0, keepdims=False)

    def in_order(own, other):
        return jnp.where(row == 0, jnp.stack([own, other]), jnp.stack([other, own]))

    def give_back(array):
        return in_order(array[:local_len], lax.ppermute(array[local_len:], "seq", across))

    both_in, normed_one_low, queries, keys, values = enter(
        inputs,
        first_gain,
        first_shift,
        query_bias,
        value_bias,
        query_weight,
        key_weight,
        value_weight,
        3,
    )
    flat_in = both_in.astype(jnp.float32)
    normed_one, norm_one_back = jax.vjp(norm_apply, flat_in, first_gain, first_shift)
    attended, log_sums, far_cot = attend(lengths, queries, keys, values, cotangent, 512, 4)
    (
        stream,
        normed_two,
        activated,
        grad_inner,
        grad_ffn,
        grad_attn,
        grad_attended,
        grad_hidden,
        sums,
    ) = feed(
        lengths,
        both_in,
        attended,
        mine_of(cotangent),
        far_cot,
        (second_gain, second_shift, output_bias, outer_bias, inner_bias),
        output_weight,
        inner_weight,
        outer_weight,
    )
    grad_outer_weight = dot(activated, grad_ffn, TN)
    grad_inner_weight = dot(normed_two, grad_inner, TN)
    grad_output_weight = dot(attended, grad_attn, TN)
    data_groups = lax.axis_size("dp")
    linked = data_groups == 8 and groups == 4
    low = jnp.bfloat16
    back_args = (lengths, queries, keys, values, grad_attended, attended, log_sums, 512)
    grads_early = (
        grad_outer_weight.astype(low),
        grad_inner_weight.astype(low),
        grad_output_weight.astype(low),
    )
    def join(partial):
        far = lax.ppermute(partial[tokens_here:], "seq", beside)
        return (partial[:tokens_here].astype(jnp.float32) + far.astype(jnp.float32)).astype(
            jnp.bfloat16
        )

    if linked:
        (grad_q_tok, grad_k_tok, grad_v_tok), other_result, sums_early = attend_back_reduce(
            *back_args, stream[local_len:], grads_early, EARLY, 2
        )
        result = in_order(stream[:local_len], other_result)
    else:
        grad_q_tok, grad_k_part, grad_v_part = attend_back(*back_args)
        grad_k_tok, grad_v_tok = join(grad_k_part), join(grad_v_part)

    grads_late = tuple(
        dot(normed_one_low, grad, TN).astype(low) for grad in (grad_q_tok, grad_k_tok, grad_v_tok)
    )
    grad_query_bias = jnp.sum(grad_q_tok, axis=0, dtype=jnp.float32)
    grad_value_bias = jnp.sum(grad_v_tok, axis=0, dtype=jnp.float32)
    grad_normed_one = (
        jnp.einsum("te,de->td", grad_q_tok, query_weight, preferred_element_type=jnp.float32)
        + jnp.einsum("te,de->td", grad_k_tok, key_weight, preferred_element_type=jnp.float32)
        + jnp.einsum("te,de->td", grad_v_tok, value_weight, preferred_element_type=jnp.float32)
    )
    grad_in_norm, grad_first_gain, grad_first_shift = norm_one_back(grad_normed_one)
    grad_in = (grad_hidden + grad_in_norm).astype(jnp.bfloat16)
    packed = jnp.concatenate(
        [
            sums,
            jnp.stack([grad_first_gain, grad_first_shift, grad_query_bias, grad_value_bias]),
        ]
    )
    if linked:
        sums_late, packed, other_in = reduce_all(grads_late, LATE, packed, grad_in[local_len:], 1)
        grad_inputs = in_order(grad_in[:local_len], other_in)
    else:

        def reduced(partial):
            piece = lax.psum_scatter(partial, ("dp", "seq"), scatter_dimension=0, tiled=True)
            return lax.all_gather(piece, "seq", axis=0, tiled=True).astype(jnp.float32)

        result = give_back(stream)
        grad_inputs = give_back(grad_in)
        sums_early = [reduced(item) for item in grads_early]
        sums_late = [reduced(item) for item in grads_late]
        packed = lax.psum(packed, ("dp", "seq"))
    summed_outer, summed_inner, summed_output = sums_early
    summed_query, summed_key, summed_value = sums_late
    inner_rows = inner_weight.shape[1] // width
    grad_inner_bias = packed[:inner_rows].reshape(-1)
    tail = packed[inner_rows:]
    denominator = tail[3, 0] * width
    stream_scale = jnp.sqrt(jnp.sum(tail[0]) / denominator)
    attention_scale = jnp.sqrt(jnp.sum(tail[1]) / denominator)
    feedforward_scale = jnp.sqrt(jnp.sum(tail[2]) / denominator)
    return (
        result,
        grad_inputs,
        tail[8],
        tail[9],
        summed_query,
        tail[10],
        summed_key,
        summed_value,
        tail[11],
        summed_output,
        tail[4],
        tail[5],
        tail[6],
        summed_inner,
        grad_inner_bias,
        summed_outer,
        tail[7],
        stream_scale,
        attention_scale,
        feedforward_scale,
    )


def solution(mesh):
    return jax.shard_map(
        local,
        mesh=mesh,
        in_specs=(
            P("dp", "seq", None),
            P("dp"),
            P(),
            P(),
            P(),
            P(),
            P(),
            P(),
            P(),
            P(),
            P(),
            P(),
            P(),
            P(),
            P(),
            P(),
            P(),
            P("dp", "seq", None),
        ),
        out_specs=(
            P("dp", "seq", None),
            P("dp", "seq", None),
            P(),
            P(),
            P("dp", None),
            P(),
            P("dp", None),
            P("dp", None),
            P(),
            P("dp", None),
            P(),
            P(),
            P(),
            P("dp", None),
            P(),
            P("dp", None),
            P(),
            P(),
            P(),
            P(),
        ),
        check_vma=False,
    )
```

profile of v0, /device:TPU:0, one launch (start us, length us, event | category | flops | bytes accessed | tf_op | source)
XLA Modules:
  0.0 337.1 jit_solution(2797325903066547172)
XLA Ops:
  0.7 2.2 dynamic-slice_bitcast_fusion.cot_ref
  3.0 0.0 copy-start.3
  3.0 1.3 copy-done.3
  4.2 1.3 copy-done.4
  5.5 27.8 %enter.1 = (bf16[1024,768]{1,0:T(8,128)(2,1)S(1)}, bf16[1024,768]{1,0:T(8,128)(2,1)}, bf16[1024,768]{1,0:T(8,128)(2,1)}, bf16[2048,768]{1,0:T(8,128)(2,1)}, bf16[2048,768]{1,0:T(8,128)(2,1)}) custom-call(bf16[2,512,768]{2,1,0:T(8,128)(2,1)} %in_ref.1, f32[1,768]{1,0:T(1,128)S(1)} %broadcast_in_dim.36.gain_ref, f32[1,768]{1,0:T(1,128)S(1)} %broadcast_in_dim.37.shift_ref, ...), custom_call_target="tpu_custom_call" | custom-call | tf_op jit(solution)/shard_map/enter/pallas_call | solution.py:437
  33.3 1.1 copy-done
  34.5 1.4 copy-done.7
  35.9 49.0 %attend.1 = (bf16[1024,768]{1,0:T(8,128)(2,1)S(1)}, f32[6,2,1024]{2,1,0:T(2,128)S(1)}, bf16[512,768]{1,0:T(8,128)(2,1)S(1)}) custom-call(s32[2]{0:T(128)S(1)} %copy-done.8, bf16[1024,768]{1,0:T(8,128)(2,1)S(1)} %copy-done.7, bf16[2048,768]{1,0:T(8,128)(2,1)} %get-tuple-element.59.k_ref.refs_2_, bf16[2048,768]{1,0:T(8,128)(2,1)} %get-tuple-element.60.v_ref.refs_3_, ...), custom_call_target="tpu_custom_call" | custom-call | flops 25769803776 | bytes 8388608 | tf_op jit(solution)/shard_map/attend/pallas_call | solution.py:94
  84.9 1.1 copy-done.9
  86.1 0.9 copy-done.11
  86.9 0.6 copy-done.12
  87.6 0.6 broadcast_in_dim.40.gain_ref
  88.1 0.6 broadcast_in_dim.41.shift_ref
  88.7 0.6 broadcast_in_dim.42.out_bias_ref
  89.3 0.6 broadcast_in_dim.43.outer_bias_ref
  89.9 51.1 %feed.1 = (bf16[1024,768]{1,0:T(8,128)(2,1)}, bf16[1024,768]{1,0:T(8,128)(2,1)}, bf16[1024,3072]{1,0:T(8,128)(2,1)}, bf16[1024,3072]{1,0:T(8,128)(2,1)}, bf16[10...) custom-call(s32[2]{0:T(128)} %refs_0_.1, ...), custom_call_target="tpu_custom_call" | custom-call | flops 21743271936 | bytes 33554432 | tf_op jit(solution)/shard_map/feed/pallas_call | solution.py:804
  141.1 4.0 %convolution_convert_fusion.5.refs_10_ = bf16[768,768]{1,0:T(8,128)(2,1)} fusion(bf16[1024,768]{1,0:T(8,128)(2,1)S(1)} %copy-done.10, bf16[1024,768]{1,0:T(8,128)(2,1)} %get-tuple-element.70), kind=kOutput, calls=%fused_computation.24 | convolution fusion | flops 1208549376 | bytes 4325376 | tf_op jit(solution)/shard_map/dot_general | solution.py:28
  145.1 8.4 %convolution_convert_fusion.refs_9_ = bf16[768,3072]{1,0:T(8,128)(2,1)} fusion(bf16[1024,768]{1,0:T(8,128)(2,1)} %get-tuple-element.68, bf16[1024,3072]{1,0:T(8,128)(2,1)S(1)} %copy-done.36), kind=kOutput, calls=%fused_computation | convolution fusion | flops 4834197504 | bytes 12582912 | tf_op jit(solution)/shard_map/dot_general | solution.py:28
  153.5 6.9 %convolution_convert_fusion.1.refs_8_ = bf16[3072,768]{1,0:T(8,128)(2,1)} fusion(bf16[1024,3072]{1,0:T(8,128)(2,1)S(1)} %bitcast.52, bf16[1024,768]{1,0:T(8,128)(2,1)S(1)} %copy-done.37), kind=kOutput, calls=%fused_computation.1 | convolution fusion | flops 4834197504 | bytes 12582912 | tf_op jit(solution)/shard_map/dot_general | solution.py:28
  160.4 1.0 slice_bitcast_fusion.1
  161.4 97.9 %attend_back_reduce.1 = (bf16[1024,768]{1,0:T(8,128)(2,1)}, bf16[1024,768]{1,0:T(8,128)(2,1)}, bf16[1024,768]{1,0:T(8,128)(2,1)}, bf16[2,192,384]{2,1,0:T(8,128)...) custom-call(s32[2]{0:T(128)} %refs_0_.1, ...), custom_call_target="tpu_custom_call" | custom-call | flops 64424509440 | bytes 33554432 | tf_op jit(solution)/shard_map/attend_back_reduce/pallas_call | solution.py:646
  259.3 3.8 %fusion.8 = f32[1024,768]{1,0:T(8,128)S(1)} fusion(bf16[768,768]{1,0:T(8,128)(2,1)} %wk_ref.1, bf16[1024,768]{1,0:T(8,128)(2,1)} %get-tuple-element.75, bf16[1024,768]{1,0:T(8,128)(2,1)} %get-tuple-element.74), kind=kOutput, calls=%fused_computation.28 | convolution fusion | flops 1211105280 | bytes 7471104 | tf_op jit(solution)/shard_map/te,de->td/dot_general | solution.py:960
  263.2 1.4 fusion.11
  264.6 0.3 convert_reduce_fusion
  264.9 0.1 copy-done.14
  265.0 1.1 copy-done.13
  266.1 2.1 fusion.5
  268.3 2.0 fusion.10
  270.3 1.3 add_convert_fusion
  271.6 1.0 slice_bitcast_fusion
  272.6 0.7 convert_reduce_fusion.1
  273.3 0.1 copy-done.25
  273.5 4.0 %convolution_convert_fusion.2.refs_2_ = bf16[768,768]{1,0:T(8,128)(2,1)S(1)} fusion(bf16[1024,768]{1,0:T(8,128)(2,1)} %get-tuple-element.78, bf16[1024,768]{1,0:T(8,128)(2,1)} %get-tuple-element.77, bf16[1024,768]{1,0:T(8,128)(2,1)} %get-tuple-element.76), kind=kOutput, calls=%fused_computation.21 | convolution fusion | flops 1211695104 | bytes 5898240 | tf_op jit(solution)/shard_map/dot_general | solution.py:28
  277.5 1.5 convolution_convert_fusion.3.refs_1_
  278.9 1.4 convolution_convert_fusion.4.refs_0_
  280.4 37.9 %reduce_all.1 = (bf16[2,48,384]{2,1,0:T(8,128)(2,1)S(1)}, bf16[2,48,384]{2,1,0:T(8,128)(2,1)S(1)}, bf16[2,48,384]{2,1,0:T(8,128)(2,1)S(1)}, bf16[2,48,384]{2,1,0...) custom-call(bf16[768,768]{1,0:T(8,128)(2,1)S(1)} %convolution_conver, ...), custom_call_target="tpu_custom_call" | custom-call | flops 17179869184 | bytes 16777216 | tf_op jit(solution)/shard_map/reduce_all/pallas_call | solution.py:545
  318.3 0.7 slice_reduce_fusion
  319.1 0.5 slice.78
  322.3 1.1 broadcast_select_fusion.1
  323.4 1.1 maximum_convert_fusion.1
  324.6 1.1 maximum_convert_fusion
  325.7 0.7 maximum_convert_fusion.5
  326.5 0.7 maximum_convert_fusion.4
  327.3 0.7 maximum_convert_fusion.3
  328.0 0.7 maximum_convert_fusion.2
  328.8 1.4 maximum_select_fusion.1
  330.1 0.6 reshape.128
  330.8 2.8 maximum_select_fusion
  (88 shorter events, 0.4 us)
Async XLA Ops:
  0.7 2.2 copy-start.24
  0.7 2.2 copy-start.26
  0.7 2.2 copy-start.27
  0.7 2.2 copy-start.28
  0.7 2.3 copy-start.2
  3.0 1.3 copy-start.3
  4.2 1.3 copy-start.4
  5.5 29.0 %copy-start.6 = (bf16[2,512,768]{2,1,0:T(8,128)(2,1)S(1)}, bf16[2,512,768]{2,1,0:T(8,128)(2,1)}, u32[]{:S(2)}) copy-start(bf16[2,512,768]{2,1,0:T(8,128)(2,1)} %cot_ref.1) | copy-start | bytes 4718596
  5.5 29.0 %copy-start.8 = (s32[2]{0:T(128)S(1)}, s32[2]{0:T(128)}, u32[]{:S(2)}) copy-start(s32[2]{0:T(128)} %refs_0_.1) | copy-start | bytes 28
  33.3 1.1 copy-start
  34.5 1.4 copy-start.7
  35.9 51.7 %copy-start.29 = (f32[768]{0:T(1024)S(1)}, f32[768]{0:T(1024)}, u32[]{:S(2)}) copy-start(f32[768]{0:T(1024)} %param.29) | copy-start | bytes 9220
  35.9 52.3 %copy-start.30 = (f32[768]{0:T(1024)S(1)}, f32[768]{0:T(1024)}, u32[]{:S(2)}) copy-start(f32[768]{0:T(1024)} %param.30) | copy-start | bytes 9220
  35.9 52.8 %copy-start.31 = (f32[768]{0:T(1024)S(1)}, f32[768]{0:T(1024)}, u32[]{:S(2)}) copy-start(f32[768]{0:T(1024)} %param.28) | copy-start | bytes 9220
  35.9 53.4 %copy-start.32 = (f32[768]{0:T(1024)S(1)}, f32[768]{0:T(1024)}, u32[]{:S(2)}) copy-start(f32[768]{0:T(1024)} %param.34) | copy-start | bytes 9220
  84.9 1.1 copy-start.9
  86.1 0.9 copy-start.11
  86.9 0.6 copy-start.12
  89.9 51.1 %copy-start.10 = (bf16[1024,768]{1,0:T(8,128)(2,1)S(1)}, bf16[1024,768]{1,0:T(8,128)(2,1)}, u32[]{:S(2)}) copy-start(bf16[1024,768]{1,0:T(8,128)(2,1)} %copy-done.9) | copy-start | bytes 4718596
  141.0 4.0 %copy-start.36 = (bf16[1024,3072]{1,0:T(8,128)(2,1)S(1)}, bf16[1024,3072]{1,0:T(8,128)(2,1)}, u32[]{:S(2)}) copy-start(bf16[1024,3072]{1,0:T(8,128)(2,1)} %get-tuple-element.69) | copy-start | bytes 18874372
  141.1 12.5 %slice-start = ((s8[6291456]{0:T(1024)(128)(4,1)}), s8[4194304]{0:T(1024)(128)(4,1)S(1)}, s32[]{:S(2)}) async-start(s8[6291456]{0:T(1024)(128)(4,1)} %bitcast.51), calls=%async_computation | async-start | bytes 8388608
  145.1 8.4 %slice-start.1 = ((s8[6291456]{0:T(1024)(128)(4,1)}), s8[2097152]{0:T(1024)(128)(4,1)S(1)}, s32[]{:S(2)}) async-start(s8[6291456]{0:T(1024)(128)(4,1)} %bitcast.51), calls=%async_computation.1 | async-start | bytes 4194304
  145.1 8.4 %copy-start.37 = (bf16[1024,768]{1,0:T(8,128)(2,1)S(1)}, bf16[1024,768]{1,0:T(8,128)(2,1)}, u32[]{:S(2)}) copy-start(bf16[1024,768]{1,0:T(8,128)(2,1)} %get-tuple-element.67) | copy-start | bytes 4718596
  153.5 6.9 %copy-start.17 = (bf16[1024,768]{1,0:T(8,128)(2,1)S(1)}, bf16[1024,768]{1,0:T(8,128)(2,1)}, u32[]{:S(2)}) copy-start(bf16[1024,768]{1,0:T(8,128)(2,1)} %get-tuple-element.63) | copy-start | bytes 4718596
  259.3 3.8 %copy-start.5 = (bf16[768,768]{1,0:T(8,128)(2,1)S(1)}, bf16[768,768]{1,0:T(8,128)(2,1)}, u32[]{:S(2)}) copy-start(bf16[768,768]{1,0:T(8,128)(2,1)} %wq_ref.1) | copy-start | bytes 3538948
  259.3 3.8 %copy-start.18 = (bf16[1024,768]{1,0:T(8,128)(2,1)S(1)}, bf16[1024,768]{1,0:T(8,128)(2,1)}, u32[]{:S(2)}) copy-start(bf16[1024,768]{1,0:T(8,128)(2,1)} %get-tuple-element.73) | copy-start | bytes 4718596
  263.2 1.5 copy-start.1
  263.2 1.9 copy-start.14
  264.6 1.5 copy-start.13
  268.3 2.0 copy-start.15
  272.6 0.8 copy-start.25
  273.4 4.0 %copy-start.33 = (bf16[1024,768]{1,0:T(8,128)(2,1)S(1)}, bf16[1024,768]{1,0:T(8,128)(2,1)}, u32[]{:S(2)}) copy-start(bf16[1024,768]{1,0:T(8,128)(2,1)} %get-tuple-element.78) | copy-start | bytes 4718596
  273.4 4.0 %copy-start.34 = (bf16[1024,768]{1,0:T(8,128)(2,1)S(1)}, bf16[1024,768]{1,0:T(8,128)(2,1)}, u32[]{:S(2)}) copy-start(bf16[1024,768]{1,0:T(8,128)(2,1)} %get-tuple-element.74) | copy-start | bytes 4718596
  273.5 4.0 %copy-start.35 = (bf16[1024,768]{1,0:T(8,128)(2,1)S(1)}, bf16[1024,768]{1,0:T(8,128)(2,1)}, u32[]{:S(2)}) copy-start(bf16[1024,768]{1,0:T(8,128)(2,1)} %get-tuple-element.75) | copy-start | bytes 4718596
  277.5 1.5 copy-start.19
  318.3 6.2 %copy-start.20 = (bf16[2,48,1536]{2,1,0:T(8,128)(2,1)S(1)}, bf16[2,48,1536]{2,1,0:T(8,128)(2,1)}, u32[]{:S(2)}) copy-start(bf16[2,48,1536]{2,1,0:T(8,128)(2,1)} %get-tuple-element.90) | copy-start | bytes 884740
  318.3 6.2 %copy-start.21 = (bf16[2,48,1536]{2,1,0:T(8,128)(2,1)S(1)}, bf16[2,48,1536]{2,1,0:T(8,128)(2,1)}, u32[]{:S(2)}) copy-start(bf16[2,48,1536]{2,1,0:T(8,128)(2,1)} %get-tuple-element.91) | copy-start | bytes 884740
  324.5 1.2 copy-start.22
  324.5 1.2 copy-start.23
  325.7 3.0 copy-start.16
where the time goes:
time: 336 us; the launch traced here: 337 us
  Pallas kernels  264 us (79%)
  matrix products  33.6 us (10%)
  local copies, waits for them, and re-layouts  16.8 us (5%)
  other arithmetic  15.5 us (5%)
  between operations  7.55 us (2%)
    pallas_call x1, Pallas kernels, attend_back_reduce(): pl.pallas_call(functools.partial(attend_back_reduce_body, len(arrays), or...  97.9 us
    pallas_call x1, Pallas kernels, feed(): pl.pallas_call(feed_body, grid_spec=pltpu.PrefetchScalarGridSpec(num_scal...  51.1 us
    pallas_call x1, Pallas kernels, attend(): pl.pallas_call(attend_body, grid_spec=pltpu.PrefetchScalarGridSpec(num_sc...  49 us
    pallas_call x1, Pallas kernels, reduce_all(): pl.pallas_call(functools.partial(reduce_body, len(arrays), orders), out_s...  37.9 us
    pallas_call x1, Pallas kernels, enter(): pl.pallas_call(enter_body, out_shape=[made(2), made(2), made(2), made(4),...  27.8 us
    dot_general x6, matrix products, dot(): lax.dot_general(left, right, (dims, ((), ())), preferred_element_type=jnp...  26.2 us
    unnamed x80, local copies, waits for them, and re-layouts  9.15 us

commit v1 on v0

--- a/solution.py
+++ b/solution.py
@@ -38,17 +38,29 @@
     return lengths_ref[lax.axis_index("seq") // 2]
 
 
-def key_valid(lengths_ref, keys_total):
-    block = keys_total // 4
-    spots = lax.broadcasted_iota(jnp.int32, (keys_total, 1), 0)
+def fill_bias(lengths_ref, bias_ref):
+    total = bias_ref.shape[0]
+    block = total // 4
+    spots = lax.broadcasted_iota(jnp.int32, (total, 1), 0)
     shift = 0
     for index, place in enumerate(block_places()):
         shift = jnp.where(spots >= index * block, (place - index) * block, shift)
-    return spots + shift < own_length(lengths_ref)
+    bias = jnp.where(spots + shift < own_length(lengths_ref), 0.0, NEGATIVE)
+    bias_ref[...] = jnp.broadcast_to(bias, bias_ref.shape).astype(jnp.bfloat16)
+
+
+def masked_scores(keys, bias, queries, head):
+    lane = lax.broadcasted_iota(jnp.int32, (1, PAIR), 1)
+    spare = HEAD_DIM * (1 - head)
+    mine = (lane < HEAD_DIM) if head == 0 else (lane >= HEAD_DIM)
+    ones = jnp.where(lane == spare, 1.0, 0.0).astype(jnp.bfloat16)
+    left = jnp.where(lane == spare, bias, keys)
+    right = jnp.where(mine, queries, jnp.broadcast_to(ones, queries.shape))
+    return dot(left, right, NT)
 
 
 def attend_body(
-    info_ref, q_ref, k_ref, v_ref, cot_ref, out_ref, lse_ref, far_ref, swap_sems
+    lengths_ref, q_ref, k_ref, v_ref, cot_ref, out_ref, lse_ref, far_ref, bias_ref, swap_sems
 ):
     bits, across = where_am_i()
     swap = swap_copy(cot_ref.at[1 - bits["y"]], far_ref, swap_sems, across)
@@ -58,18 +70,16 @@
     def _():
         greet(across, ("y",))
         swap.start()
-
-    lane = lax.broadcasted_iota(jnp.int32, (1, PAIR), 1)
+        fill_bias(lengths_ref, bias_ref)
+
     scale = jnp.bfloat16(HEAD_DIM ** (-0.5))
     queries = q_ref[...] * scale
     keys = k_ref[...]
     values_t = v_ref[...].T
-    valid = key_valid(info_ref, keys.shape[0])
+    bias = bias_ref[...]
     outs = []
     for head in range(2):
-        mine = (lane < HEAD_DIM) if head == 0 else (lane >= HEAD_DIM)
-        scores = dot(keys, jnp.where(mine, queries, jnp.zeros_like(queries)), NT)
-        scores = jnp.where(valid, scores, NEGATIVE)
+        scores = masked_scores(keys, bias, queries, head)
         top = jnp.max(scores, axis=0, keepdims=True)
         weights = jnp.exp(scores - top)
         total = jnp.sum(weights, axis=0, keepdims=True)
@@ -102,7 +112,10 @@
                 pl.BlockSpec((1, 2, block), lambda h, i, n: (h, 0, i)),
                 pl.BlockSpec(memory_space=pl.ANY),
             ],
-            scratch_shapes=[pltpu.SemaphoreType.DMA((2,))],
+            scratch_shapes=[
+                pltpu.VMEM((total, PAIR), jnp.bfloat16),
+                pltpu.SemaphoreType.DMA((2,)),
+            ],
         ),
         out_shape=[
             jax.ShapeDtypeStruct((tokens, width), jnp.bfloat16),
@@ -120,7 +133,7 @@
 
 
 def attend_back_body(
-    info_ref,
+    lengths_ref,
     q_ref,
     k_ref,
     v_ref,
@@ -130,12 +143,18 @@
     dq_ref,
     dk_ref,
     dv_ref,
+    bias_ref,
     dk_acc,
     dv_acc,
     before=None,
     after=None,
 ):
     step = pl.program_id(1)
+
+    @pl.when((step == 0) & (pl.program_id(0) == 0))
+    def _():
+        fill_bias(lengths_ref, bias_ref)
+
     lane = lax.broadcasted_iota(jnp.int32, (1, PAIR), 1)
     scale = jnp.bfloat16(HEAD_DIM ** (-0.5))
     grad_out = do_ref[...]
@@ -155,7 +174,7 @@
         precision=lax.Precision.HIGHEST,
         preferred_element_type=jnp.float32,
     )
-    valid = key_valid(info_ref, keys.shape[0])
+    bias = bias_ref[...]
     zero = jnp.zeros_like(queries)
     grad_k = 0
     grad_v = 0
@@ -166,7 +185,7 @@
         mine = (lane < HEAD_DIM) if head == 0 else (lane >= HEAD_DIM)
         query_h = jnp.where(mine, queries, zero)
         out_h = jnp.where(mine, grad_out, zero)
-        scores = jnp.where(valid, dot(keys, query_h, NT), NEGATIVE)
+        scores = masked_scores(keys, bias, queries, head)
         weights = jnp.exp(scores - lse_ref[0, head : head + 1, :])
         grad_w = dot(values, out_h, NT)
         grad_s = (weights * (grad_w - row_sums[head : head + 1])).astype(jnp.bfloat16)
@@ -215,7 +234,11 @@
                 pl.BlockSpec((1, 2, block), lambda h, i, n: (h, 0, i)),
             ],
             out_specs=[q_spec, k_spec, k_spec],
-            scratch_shapes=[pltpu.VMEM((total, PAIR), jnp.float32)] * 2,
+            scratch_shapes=[
+                pltpu.VMEM((total, PAIR), jnp.bfloat16),
+                pltpu.VMEM((total, PAIR), jnp.float32),
+                pltpu.VMEM((total, PAIR), jnp.float32),
+            ],
         ),
         out_shape=[
             jax.ShapeDtypeStruct((tokens, width), jnp.bfloat16),
@@ -568,7 +591,8 @@
     outs = refs[11 + count : 11 + 3 * count]
     far = refs[11 + 3 * count : 13 + 3 * count]
     swap_out = refs[13 + 3 * count]
-    dk_acc, dv_acc, send_k, send_v, trade_sems, swap_sems, *scratch = refs[14 + 3 * count :]
+    bias_ref, dk_acc, dv_acc, *scratch = refs[14 + 3 * count :]
+    send_k, send_v, trade_sems, swap_sems, *scratch = scratch
     pair = pl.program_id(0)
     pairs = pl.num_programs(0)
     now = 2 * (pair * pl.num_programs(1) + pl.program_id(1))
@@ -612,7 +636,7 @@
         trade(pair, 0).start()
         trade(pair, 1).start()
 
-    attend_back_body(info_ref, *blocks, *results, dk_acc, dv_acc, before, after)
+    attend_back_body(info_ref, *blocks, *results, bias_ref, dk_acc, dv_acc, before, after)
 
     @pl.when(now + 2 == last)
     def _():
@@ -659,6 +683,7 @@
             ],
             out_specs=[q_spec, near_spec, near_spec, *[whole] * len(outs), *[anywhere] * 3],
             scratch_shapes=[
+                pltpu.VMEM((total, PAIR), jnp.bfloat16),
                 pltpu.VMEM((total, PAIR), jnp.float32),
                 pltpu.VMEM((total, PAIR), jnp.float32),
                 pltpu.VMEM((pairs, near, PAIR), jnp.bfloat16),
@@ -694,6 +719,82 @@
 
 
 def feed_body(
+    lengths_ref,
+    x_ref,
+    att_ref,
+    cot_ref,
+    cot_far_ref,
+    gain_ref,
+    shift_ref,
+    out_bias_ref,
+    outer_bias_ref,
+    inner_bias_ref,
+    wo_ref,
+    wi_ref,
+    wf_ref,
+    result_ref,
+    g_att_ref,
+    g_hidden_ref,
+    sums_ref,
+    g_wf_ref,
+    g_wi_ref,
+    g_wo_ref,
+    act_all,
+    g_inner_all,
+    normed_all,
+    g_ffn_all,
+    att_all,
+    g_attn_all,
+):
+    step = pl.program_id(0)
+    block, width = x_ref.shape
+    chunks = wi_ref.shape[1] // width
+
+    @pl.when(step < 2)
+    def _():
+        span = pl.ds(pl.multiple_of(step * block, block), block)
+        att_all[span, :] = att_ref[...]
+        feed_block(
+            lengths_ref,
+            x_ref,
+            att_ref,
+            cot_ref,
+            cot_far_ref,
+            gain_ref,
+            shift_ref,
+            out_bias_ref,
+            outer_bias_ref,
+            inner_bias_ref,
+            wo_ref,
+            wi_ref,
+            wf_ref,
+            result_ref,
+            normed_all.at[span],
+            act_all.at[span],
+            g_inner_all.at[span],
+            g_ffn_all.at[span],
+            g_attn_all.at[span],
+            g_att_ref,
+            g_hidden_ref,
+            sums_ref,
+        )
+
+    @pl.when((step >= 2) & (step < 2 + chunks))
+    def _():
+        span = pl.ds(pl.multiple_of((step - 2) * width, width), width)
+        g_wf_ref[...] = dot(act_all[:, span], g_ffn_all[...], TN).astype(jnp.bfloat16)
+
+    @pl.when((step >= 2 + chunks) & (step < 2 + 2 * chunks))
+    def _():
+        span = pl.ds(pl.multiple_of((step - 2 - chunks) * width, width), width)
+        g_wi_ref[...] = dot(normed_all[...], g_inner_all[:, span], TN).astype(jnp.bfloat16)
+
+    @pl.when(step == 2 + 2 * chunks)
+    def _():
+        g_wo_ref[...] = dot(att_all[...], g_attn_all[...], TN).astype(jnp.bfloat16)
+
+
+def feed_block(
     lengths_ref,
     x_ref,
     att_ref,
@@ -794,18 +895,18 @@
     inner_total = wi.shape[1]
     low = jnp.bfloat16
     block = tokens // 2
-    slot = pl.BlockSpec((block, width), lambda i, n: (i, 0))
-    wide = pl.BlockSpec((block, inner_total), lambda i, n: (i, 0))
+    chunks = inner_total // width
+    slot = pl.BlockSpec((block, width), lambda i, n: (jnp.minimum(i, 1), 0))
 
     def fixed(shape):
         return pl.BlockSpec(shape, lambda i, n: (0, 0), pipeline_mode=pl.Buffered(1))
 
-    sums_rows = inner_total // width + 8
+    sums_rows = chunks + 8
     return pl.pallas_call(
         feed_body,
         grid_spec=pltpu.PrefetchScalarGridSpec(
             num_scalar_prefetch=1,
-            grid=(2,),
+            grid=(3 + 2 * chunks,),
             in_specs=[
                 slot,
                 slot,
@@ -819,29 +920,32 @@
             out_specs=[
                 slot,
                 slot,
-                wide,
-                wide,
-                slot,
-                slot,
-                slot,
                 slot,
                 pl.BlockSpec((sums_rows, width), lambda i, n: (0, 0)),
+                pl.BlockSpec((width, width), lambda i, n: (jnp.clip(i - 2, 0, chunks - 1), 0)),
+                pl.BlockSpec(
+                    (width, width), lambda i, n: (0, jnp.clip(i - 2 - chunks, 0, chunks - 1))
+                ),
+                pl.BlockSpec((width, width), lambda i, n: (0, 0)),
             ],
+            scratch_shapes=[
+                pltpu.VMEM((tokens, inner_total), low),
+                pltpu.VMEM((tokens, inner_total), low),
+                *[pltpu.VMEM((tokens, width), low)] * 4,
+            ],
         ),
         out_shape=[
-            jax.ShapeDtypeStruct((tokens, width), low),
-            jax.ShapeDtypeStruct((tokens, width), low),
-            jax.ShapeDtypeStruct((tokens, inner_total), low),
-            jax.ShapeDtypeStruct((tokens, inner_total), low),
-            jax.ShapeDtypeStruct((tokens, width), low),
             jax.ShapeDtypeStruct((tokens, width), low),
             jax.ShapeDtypeStruct((tokens, width), low),
             jax.ShapeDtypeStruct((tokens, width), jnp.float32),
             jax.ShapeDtypeStruct((sums_rows, width), jnp.float32),
+            jax.ShapeDtypeStruct((inner_total, width), low),
+            jax.ShapeDtypeStruct((width, inner_total), low),
+            jax.ShapeDtypeStruct((width, width), low),
         ],
-        compiler_params=pltpu.CompilerParams(vmem_limit_bytes=60 << 20),
+        compiler_params=pltpu.CompilerParams(vmem_limit_bytes=62 << 20),
         cost_estimate=pl.CostEstimate(
-            flops=4 * tokens * width * (width + 2 * inner_total),
+            flops=6 * tokens * width * (width + 2 * inner_total),
             bytes_accessed=1 << 25,
             transcendentals=0,
         ),
@@ -904,14 +1008,12 @@
     attended, log_sums, far_cot = attend(lengths, queries, keys, values, cotangent, 512, 4)
     (
         stream,
-        normed_two,
-        activated,
-        grad_inner,
-        grad_ffn,
-        grad_attn,
         grad_attended,
         grad_hidden,
         sums,
+        grad_outer_weight,
+        grad_inner_weight,
+        grad_output_weight,
     ) = feed(
         lengths,
         both_in,
@@ -923,18 +1025,11 @@
         inner_weight,
         outer_weight,
     )
-    grad_outer_weight = dot(activated, grad_ffn, TN)
-    grad_inner_weight = dot(normed_two, grad_inner, TN)
-    grad_output_weight = dot(attended, grad_attn, TN)
     data_groups = lax.axis_size("dp")
     linked = data_groups == 8 and groups == 4
     low = jnp.bfloat16
     back_args = (lengths, queries, keys, values, grad_attended, attended, log_sums, 512)
-    grads_early = (
-        grad_outer_weight.astype(low),
-        grad_inner_weight.astype(low),
-        grad_output_weight.astype(low),
-    )
+    grads_early = (grad_outer_weight, grad_inner_weight, grad_output_weight)
     def join(partial):
         far = lax.ppermute(partial[tokens_here:], "seq", beside)
         return (partial[:tokens_here].astype(jnp.float32) + far.astype(jnp.float32)).astype(

time: 336 us -> 320 us (0.952); the launches traced: 337 us -> 315 us
  matrix products: 33.6 us -> 14.2 us
  Pallas kernels: 264 us -> 260 us
    dot_general x6 -> x3, matrix products: 26.2 us -> 6.84 us  [dot(): lax.dot_general(left, right, (dims, ((), ())), preferred_element_type=jnp...]
    unnamed x80 -> x68, local copies, waits for them, and re-layouts: 9.15 us -> 9.19 us
where the time goes in v1:
time: 320 us; the launch traced here: 315 us
  Pallas kernels  260 us (81%)
  local copies, waits for them, and re-layouts  18.2 us (6%)
  other arithmetic  15.5 us (5%)
  matrix products  14.2 us (4%)
  between operations  7.46 us (2%)
    pallas_call x1, Pallas kernels, attend_back_reduce(): pl.pallas_call(functools.partial(attend_back_reduce_body, len(arrays), or...  95.8 us
    pallas_call x1, Pallas kernels, feed(): pl.pallas_call(feed_body, grid_spec=pltpu.PrefetchScalarGridSpec(num_scal...  51.2 us
    pallas_call x1, Pallas kernels, attend(): pl.pallas_call(attend_body, grid_spec=pltpu.PrefetchScalarGridSpec(num_sc...  46.9 us
    pallas_call x1, Pallas kernels, reduce_all(): pl.pallas_call(functools.partial(reduce_body, len(arrays), orders), out_s...  38 us
    pallas_call x1, Pallas kernels, enter(): pl.pallas_call(enter_body, out_shape=[made(2), made(2), made(2), made(4),...  27.9 us
    unnamed x68, local copies, waits for them, and re-layouts  9.19 us
    dot_general x3, matrix products, dot(): lax.dot_general(left, right, (dims, ((), ())), preferred_element_type=jnp...  6.84 us

profile of v1, /device:TPU:0, one launch (start us, length us, event | category | flops | bytes accessed | tf_op | source)
XLA Modules:
  0.0 315.0 jit_solution(15511898533503274030)
XLA Ops:
  0.7 2.2 dynamic-slice_bitcast_fusion.cot_ref
  3.0 0.0 copy-start.3
  3.0 1.3 copy-done.3
  4.2 1.3 copy-done.4
  5.5 27.9 %enter.1 = (bf16[1024,768]{1,0:T(8,128)(2,1)S(1)}, bf16[1024,768]{1,0:T(8,128)(2,1)}, bf16[1024,768]{1,0:T(8,128)(2,1)}, bf16[2048,768]{1,0:T(8,128)(2,1)}, bf16[2048,768]{1,0:T(8,128)(2,1)}) custom-call(bf16[2,512,768]{2,1,0:T(8,128)(2,1)} %in_ref.1, f32[1,768]{1,0:T(1,128)S(1)} %broadcast_in_dim.36.gain_ref, f32[1,768]{1,0:T(1,128)S(1)} %broadcast_in_dim.37.shift_ref, ...), custom_call_target="tpu_custom_call" | custom-call | tf_op jit(solution)/shard_map/enter/pallas_call | solution.py:460
  33.4 0.0 copy-start
  33.4 1.1 copy-done
  34.5 1.4 copy-done.7
  36.0 46.9 %attend.1 = (bf16[1024,768]{1,0:T(8,128)(2,1)S(1)}, f32[6,2,1024]{2,1,0:T(2,128)S(1)}, bf16[512,768]{1,0:T(8,128)(2,1)S(1)}) custom-call(s32[2]{0:T(128)S(1)} %copy-done.8, bf16[1024,768]{1,0:T(8,128)(2,1)S(1)} %copy-done.7, bf16[2048,768]{1,0:T(8,128)(2,1)} %get-tuple-element.57.k_ref.refs_2_, bf16[2048,768]{1,0:T(8,128)(2,1)} %get-tuple-element.58.v_ref.refs_3_, ...), custom_call_target="tpu_custom_call" | custom-call | flops 25769803776 | bytes 8388608 | tf_op jit(solution)/shard_map/attend/pallas_call | solution.py:104
  82.9 0.0 copy-start.9
  82.9 1.1 copy-done.9
  84.0 0.9 copy-done.10
  84.9 0.6 copy-done.11
  85.6 0.6 broadcast_in_dim.40.gain_ref
  86.1 0.6 broadcast_in_dim.41.shift_ref
  86.7 0.6 broadcast_in_dim.42.out_bias_ref
  87.3 0.6 broadcast_in_dim.43.outer_bias_ref
  87.9 51.2 %feed.1 = (bf16[1024,768]{1,0:T(8,128)(2,1)}, bf16[1024,768]{1,0:T(8,128)(2,1)}, f32[1024,768]{1,0:T(8,128)}, f32[12,768]{1,0:T(8,128)}, bf16[3072,768]{1,0:T(8,...) custom-call(s32[2]{0:T(128)} %refs_0_.1, bf16[1024,768]{1,0:T(8,128)(2,1)} %copy-done, ...), custom_call_target="tpu_custom_call" | custom-call | flops 32614907904 | bytes 33554432 | tf_op jit(solution)/shard_map/feed/pallas_call | solution.py:905
  139.1 2.4 slice_bitcast_fusion.1
  141.4 95.8 %attend_back_reduce.1 = (bf16[1024,768]{1,0:T(8,128)(2,1)}, bf16[1024,768]{1,0:T(8,128)(2,1)}, bf16[1024,768]{1,0:T(8,128)(2,1)}, bf16[2,192,384]{2,1,0:T(8,128)...) custom-call(s32[2]{0:T(128)} %refs_0_.1, ...), custom_call_target="tpu_custom_call" | custom-call | flops 64424509440 | bytes 33554432 | tf_op jit(solution)/shard_map/attend_back_reduce/pallas_call | solution.py:670
  237.2 3.8 %fusion.8 = f32[1024,768]{1,0:T(8,128)S(1)} fusion(bf16[768,768]{1,0:T(8,128)(2,1)} %wk_ref.1, bf16[1024,768]{1,0:T(8,128)(2,1)} %get-tuple-element.71, bf16[1024,768]{1,0:T(8,128)(2,1)} %get-tuple-element.70), kind=kOutput, calls=%fused_computation.25 | convolution fusion | flops 1211105280 | bytes 7471104 | tf_op jit(solution)/shard_map/te,de->td/dot_general | solution.py:1055
  241.0 0.0 copy-start.1
  241.1 1.4 fusion.11
  242.5 0.3 convert_reduce_fusion
  242.8 0.1 copy-done.13
  242.9 1.1 copy-done.12
  244.0 2.1 fusion.5
  246.2 2.0 fusion.10
  248.2 1.3 add_convert_fusion
  249.5 1.0 slice_bitcast_fusion
  250.5 0.7 convert_reduce_fusion.1
  251.2 0.1 copy-done.23
  251.3 4.0 %convolution_convert_fusion.refs_2_ = bf16[768,768]{1,0:T(8,128)(2,1)S(1)} fusion(bf16[1024,768]{1,0:T(8,128)(2,1)} %get-tuple-element.74, bf16[1024,768]{1,0:T(8,128)(2,1)} %get-tuple-element.73, bf16[1024,768]{1,0:T(8,128)(2,1)} %get-tuple-element.72), kind=kOutput, calls=%fused_computation.19 | convolution fusion | flops 1211695104 | bytes 5898240 | tf_op jit(solution)/shard_map/dot_general | solution.py:28
  255.3 1.4 convolution_convert_fusion.1.refs_1_
  256.8 1.4 convolution_convert_fusion.2.refs_0_
  258.3 38.0 %reduce_all.1 = (bf16[2,48,384]{2,1,0:T(8,128)(2,1)S(1)}, bf16[2,48,384]{2,1,0:T(8,128)(2,1)S(1)}, bf16[2,48,384]{2,1,0:T(8,128)(2,1)S(1)}, bf16[2,48,384]{2,1,0...) custom-call(bf16[768,768]{1,0:T(8,128)(2,1)S(1)} %convolution_conver, ...), custom_call_target="tpu_custom_call" | custom-call | flops 17179869184 | bytes 16777216 | tf_op jit(solution)/shard_map/reduce_all/pallas_call | solution.py:568
  296.3 0.7 slice_reduce_fusion
  297.0 0.5 slice.78
  300.3 1.1 broadcast_select_fusion.1
  301.4 1.1 maximum_convert_fusion.1
  302.5 1.1 maximum_convert_fusion
  303.7 0.7 maximum_convert_fusion.5
  304.4 0.7 maximum_convert_fusion.4
  305.2 0.7 maximum_convert_fusion.3
  306.0 0.7 maximum_convert_fusion.2
  306.7 1.4 maximum_select_fusion.1
  308.1 0.6 reshape.128
  308.7 2.8 maximum_select_fusion
  (72 shorter events, 0.3 us)
Async XLA Ops:
  0.7 2.2 copy-start.22
  0.7 2.2 copy-start.24
  0.7 2.2 copy-start.25
  0.7 2.2 copy-start.26
  0.7 2.3 copy-start.2
  3.0 1.3 copy-start.3
  4.2 1.3 copy-start.4
  5.5 29.0 %copy-start.6 = (bf16[2,512,768]{2,1,0:T(8,128)(2,1)S(1)}, bf16[2,512,768]{2,1,0:T(8,128)(2,1)}, u32[]{:S(2)}) copy-start(bf16[2,512,768]{2,1,0:T(8,128)(2,1)} %cot_ref.1) | copy-start | bytes 4718596
  5.5 29.0 %copy-start.8 = (s32[2]{0:T(128)S(1)}, s32[2]{0:T(128)}, u32[]{:S(2)}) copy-start(s32[2]{0:T(128)} %refs_0_.1) | copy-start | bytes 28
  33.4 1.1 copy-start
  34.5 1.4 copy-start.7
  35.9 49.6 %copy-start.27 = (f32[768]{0:T(1024)S(1)}, f32[768]{0:T(1024)}, u32[]{:S(2)}) copy-start(f32[768]{0:T(1024)} %param.29) | copy-start | bytes 9220
  35.9 50.2 %copy-start.28 = (f32[768]{0:T(1024)S(1)}, f32[768]{0:T(1024)}, u32[]{:S(2)}) copy-start(f32[768]{0:T(1024)} %param.30) | copy-start | bytes 9220
  36.0 50.8 %copy-start.29 = (f32[768]{0:T(1024)S(1)}, f32[768]{0:T(1024)}, u32[]{:S(2)}) copy-start(f32[768]{0:T(1024)} %param.28) | copy-start | bytes 9220
  36.0 51.4 %copy-start.30 = (f32[768]{0:T(1024)S(1)}, f32[768]{0:T(1024)}, u32[]{:S(2)}) copy-start(f32[768]{0:T(1024)} %param.34) | copy-start | bytes 9220
  82.9 1.1 copy-start.9
  84.0 0.9 copy-start.10
  84.9 0.6 copy-start.11
  237.2 3.8 %copy-start.5 = (bf16[768,768]{1,0:T(8,128)(2,1)S(1)}, bf16[768,768]{1,0:T(8,128)(2,1)}, u32[]{:S(2)}) copy-start(bf16[768,768]{1,0:T(8,128)(2,1)} %wq_ref.1) | copy-start | bytes 3538948
  237.2 3.8 %copy-start.16 = (bf16[1024,768]{1,0:T(8,128)(2,1)S(1)}, bf16[1024,768]{1,0:T(8,128)(2,1)}, u32[]{:S(2)}) copy-start(bf16[1024,768]{1,0:T(8,128)(2,1)} %get-tuple-element.69) | copy-start | bytes 4718596
  241.0 1.5 copy-start.1
  241.1 1.9 copy-start.13
  242.5 1.5 copy-start.12
  246.2 2.0 copy-start.14
  250.5 0.8 copy-start.23
  251.3 4.0 %copy-start.31 = (bf16[1024,768]{1,0:T(8,128)(2,1)S(1)}, bf16[1024,768]{1,0:T(8,128)(2,1)}, u32[]{:S(2)}) copy-start(bf16[1024,768]{1,0:T(8,128)(2,1)} %get-tuple-element.74) | copy-start | bytes 4718596
  251.3 4.0 %copy-start.32 = (bf16[1024,768]{1,0:T(8,128)(2,1)S(1)}, bf16[1024,768]{1,0:T(8,128)(2,1)}, u32[]{:S(2)}) copy-start(bf16[1024,768]{1,0:T(8,128)(2,1)} %get-tuple-element.70) | copy-start | bytes 4718596
  251.3 4.0 %copy-start.33 = (bf16[1024,768]{1,0:T(8,128)(2,1)S(1)}, bf16[1024,768]{1,0:T(8,128)(2,1)}, u32[]{:S(2)}) copy-start(bf16[1024,768]{1,0:T(8,128)(2,1)} %get-tuple-element.71) | copy-start | bytes 4718596
  255.3 1.5 copy-start.17
  296.2 6.2 %copy-start.18 = (bf16[2,48,1536]{2,1,0:T(8,128)(2,1)S(1)}, bf16[2,48,1536]{2,1,0:T(8,128)(2,1)}, u32[]{:S(2)}) copy-start(bf16[2,48,1536]{2,1,0:T(8,128)(2,1)} %get-tuple-element.86) | copy-start | bytes 884740
  296.3 6.2 %copy-start.19 = (bf16[2,48,1536]{2,1,0:T(8,128)(2,1)S(1)}, bf16[2,48,1536]{2,1,0:T(8,128)(2,1)}, u32[]{:S(2)}) copy-start(bf16[2,48,1536]{2,1,0:T(8,128)(2,1)} %get-tuple-element.87) | copy-start | bytes 884740
  302.5 1.2 copy-start.20
  302.5 1.2 copy-start.21
  303.6 3.0 copy-start.15

commit v2 on v1

--- a/solution.py
+++ b/solution.py
@@ -255,7 +255,7 @@
 
 MESH_IDS = pl.DeviceIdType.MESH
 AXES = ("zhi", "zlo", "x", "y")
-LATE = (("x", "zlo", "y", "zhi"), ("zlo", "x", "y", "zhi"), ("x", "zlo", "zhi", "y"))
+LATE = (("x", "zlo", "zhi", "y"), ("zlo", "x", "zhi", "y"), ("x", "zlo", "zhi", "y"))
 
 
 def where_am_i():
@@ -516,9 +516,7 @@
     return sums
 
 
-def vector_sum(source, held, lands, sems, bits_across):
-    bits, across = bits_across
-    held[...] = source[...]
+def vector_sum(held, lands, sems, across):
     for slot, axis in enumerate(("core", "y", "x", "zlo", "zhi")):
         copy = pltpu.make_async_remote_copy(
             src_ref=held,
@@ -534,22 +532,73 @@
         held[...] = held[...] + lands[slot]
 
 
-def reduce_body(count, orders, *refs):
-    sources, vector, far = refs[:count], refs[count], refs[count + 1]
-    outs = refs[count + 2 : count + 2 + 2 * count]
-    vector_out, far_out = refs[3 * count + 2 : 3 * count + 4]
-    swap_sems, *scratch = refs[3 * count + 4 :]
+def leave_body(
+    orders,
+    x_ref,
+    normed_ref,
+    gq_ref,
+    gk_ref,
+    gk_far_ref,
+    gv_ref,
+    gv_far_ref,
+    g_hidden_ref,
+    gain_ref,
+    wq_ref,
+    wk_ref,
+    wv_ref,
+    sums_ref,
+    *refs,
+):
+    outs = refs[:6]
+    vector_ref, grad_ref, far_ref = refs[6:9]
+    gk_all, gv_all, *products = refs[9:14]
+    vector_lands, vector_sems, swap_sems, *scratch = refs[14:]
+    low = jnp.bfloat16
     bits, across = where_am_i()
+    colors = colors_of(products, scratch, orders)
+    gk_all[...] = (gk_ref[...].astype(jnp.float32) + gk_far_ref[...].astype(jnp.float32)).astype(low)
+    gv_all[...] = (gv_ref[...].astype(jnp.float32) + gv_far_ref[...].astype(jnp.float32)).astype(low)
     greet(across)
-    swap = swap_copy(far, far_out, swap_sems, across)
-    swap.start()
-    colors = colors_of(sources, scratch, orders)
-    vector_lands, vector_sems = scratch[9 * count :]
-    small = vector_sum(vector, vector_out, vector_lands, vector_sems, (bits, across))
-    for color in colors:
+    for product, grads, color in zip(products, (gq_ref, gk_all, gv_all), colors):
+        product[...] = dot(normed_ref[...], grads[...], TN).astype(low)
         color.begin()
+    colors[0].step(0)
+    colors[1].step(0)
+    count = x_ref.shape[0] // 2
+    swap = swap_copy(grad_ref.at[pl.ds(count, count)], far_ref, swap_sems, across)
+    early = sums_ref.shape[0]
+    vector_ref[:early] = sums_ref[...]
+    vector_ref[early:] = jnp.zeros_like(vector_ref[early:])
+    gain = gain_ref[...]
+    for start in (count, 0):
+        span = slice(start, start + count)
+        rows = x_ref[span].astype(jnp.float32)
+        centered = rows - jnp.mean(rows, axis=-1, keepdims=True)
+        spread = lax.rsqrt(jnp.mean(centered * centered, axis=-1, keepdims=True) + EPSILON)
+        normal = centered * spread
+        gq, gv = gq_ref[span], gv_all[span]
+        g_normed = (
+            dot(gq, wq_ref[...], NT)
+            + dot(gk_all[span], wk_ref[...], NT)
+            + dot(gv, wv_ref[...], NT)
+        )
+        e = g_normed * gain
+        g_rows = spread * (
+            e
+            - jnp.mean(e, axis=-1, keepdims=True)
+            - normal * jnp.mean(e * normal, axis=-1, keepdims=True)
+        )
+        grad_ref[span] = (g_hidden_ref[span] + g_rows).astype(low)
+        if start:
+            swap.start()
+            colors[2].step(0)
+        late = [g_normed * normal, g_normed, gq.astype(jnp.float32), gv.astype(jnp.float32)]
+        vector_ref[early:] += jnp.concatenate(
+            [jnp.sum(item, axis=0, keepdims=True) for item in late], axis=0
+        )
+    small = vector_sum(vector_ref, vector_lands, vector_sems, across)
     next(small)
-    for stage in range(7):
+    for stage in range(1, 7):
         for color in colors:
             color.step(stage)
         next(small, None)
@@ -557,27 +606,38 @@
     swap.wait()
 
 
-def reduce_all(arrays, orders, vector, far, collective):
+def leave(x, normed, gq, gks, gvs, g_hidden, gain, wq, wk, wv, sums, orders, collective):
+    tokens, width = x.shape
+    vmem = pl.BlockSpec(memory_space=pltpu.VMEM)
+    square = jax.ShapeDtypeStruct((width, width), jnp.bfloat16)
+    arrays = (square,) * 3
     scratch, outs = color_scratch(arrays)
-    scratch.append(pltpu.VMEM((5, *vector.shape), jnp.float32))
-    scratch.append(pltpu.SemaphoreType.DMA((2, 5)))
-    outs.append(jax.ShapeDtypeStruct(vector.shape, jnp.float32))
-    outs.append(jax.ShapeDtypeStruct(far.shape, far.dtype))
-    anywhere = pl.BlockSpec(memory_space=pl.ANY)
-    vmem = pl.BlockSpec(memory_space=pltpu.VMEM)
+    vector = (sums.shape[0] + 4, width)
+    outs += [
+        jax.ShapeDtypeStruct(vector, jnp.float32),
+        jax.ShapeDtypeStruct((tokens, width), jnp.bfloat16),
+        jax.ShapeDtypeStruct((tokens // 2, width), jnp.bfloat16),
+    ]
     got = pl.pallas_call(
-        functools.partial(reduce_body, len(arrays), orders),
+        functools.partial(leave_body, orders),
         out_shape=outs,
-        in_specs=[*[anywhere] * len(arrays), vmem, anywhere],
-        out_specs=[*[vmem] * (len(outs) - 1), anywhere],
-        scratch_shapes=[pltpu.SemaphoreType.DMA((2,)), *scratch],
+        in_specs=[vmem] * 13,
+        out_specs=[*[vmem] * (len(outs) - 1), pl.BlockSpec(memory_space=pl.ANY)],
+        scratch_shapes=[
+            *[pltpu.VMEM((tokens, width), jnp.bfloat16)] * 2,
+            *[pltpu.VMEM((width, width), jnp.bfloat16)] * 3,
+            pltpu.VMEM((5, *vector), jnp.float32),
+            pltpu.SemaphoreType.DMA((2, 5)),
+            pltpu.SemaphoreType.DMA((2,)),
+            *scratch,
+        ],
         compiler_params=pltpu.CompilerParams(
-            collective_id=collective, has_side_effects=True, vmem_limit_bytes=40 << 20
+            collective_id=collective, has_side_effects=True, vmem_limit_bytes=56 << 20
         ),
         cost_estimate=pl.CostEstimate(flops=1 << 34, bytes_accessed=1 << 24, transcendentals=0),
-        name="reduce_all",
-    )(*arrays, vector, far)
-    return assemble(arrays, got), got[-2], got[-1]
+        name="leave",
+    )(x, normed, gq, *gks, *gvs, g_hidden, gain[None], wq, wk, wv, sums)
+    return assemble(arrays, got), got[6], got[7], got[8]
 
 
 TIMES = ((3, 11, 15, 17, 20, 22, 24), (4, 12, 16, 18, 21, 22, 24), (5, 8, 10, 13, 16, 19, 21))
@@ -711,10 +771,7 @@
         name="attend_back_reduce",
     )(info, queries, keys, values, grad_out, out, log_sums, swap, *arrays)
 
-    def joined(own, other):
-        return (own.astype(jnp.float32) + other.astype(jnp.float32)).astype(jnp.bfloat16)
-
-    grads = (got[0], joined(got[1], got[-3]), joined(got[2], got[-2]))
+    grads = (got[0], (got[1], got[-3]), (got[2], got[-2]))
     return grads, got[-1], assemble(arrays, got[3:-3])
 
 
@@ -1003,8 +1060,6 @@
         value_weight,
         3,
     )
-    flat_in = both_in.astype(jnp.float32)
-    normed_one, norm_one_back = jax.vjp(norm_apply, flat_in, first_gain, first_shift)
     attended, log_sums, far_cot = attend(lengths, queries, keys, values, cotangent, 512, 4)
     (
         stream,
@@ -1030,53 +1085,54 @@
     low = jnp.bfloat16
     back_args = (lengths, queries, keys, values, grad_attended, attended, log_sums, 512)
     grads_early = (grad_outer_weight, grad_inner_weight, grad_output_weight)
-    def join(partial):
-        far = lax.ppermute(partial[tokens_here:], "seq", beside)
-        return (partial[:tokens_here].astype(jnp.float32) + far.astype(jnp.float32)).astype(
-            jnp.bfloat16
-        )
 
     if linked:
-        (grad_q_tok, grad_k_tok, grad_v_tok), other_result, sums_early = attend_back_reduce(
+        (grad_q, grads_k, grads_v), other_result, sums_early = attend_back_reduce(
             *back_args, stream[local_len:], grads_early, EARLY, 2
         )
         result = in_order(stream[:local_len], other_result)
-    else:
-        grad_q_tok, grad_k_part, grad_v_part = attend_back(*back_args)
-        grad_k_tok, grad_v_tok = join(grad_k_part), join(grad_v_part)
-
-    grads_late = tuple(
-        dot(normed_one_low, grad, TN).astype(low) for grad in (grad_q_tok, grad_k_tok, grad_v_tok)
-    )
-    grad_query_bias = jnp.sum(grad_q_tok, axis=0, dtype=jnp.float32)
-    grad_value_bias = jnp.sum(grad_v_tok, axis=0, dtype=jnp.float32)
-    grad_normed_one = (
-        jnp.einsum("te,de->td", grad_q_tok, query_weight, preferred_element_type=jnp.float32)
-        + jnp.einsum("te,de->td", grad_k_tok, key_weight, preferred_element_type=jnp.float32)
-        + jnp.einsum("te,de->td", grad_v_tok, value_weight, preferred_element_type=jnp.float32)
-    )
-    grad_in_norm, grad_first_gain, grad_first_shift = norm_one_back(grad_normed_one)
-    grad_in = (grad_hidden + grad_in_norm).astype(jnp.bfloat16)
-    packed = jnp.concatenate(
-        [
+        sums_late, packed, grad_in, other_in = leave(
+            both_in,
+            normed_one_low,
+            grad_q,
+            grads_k,
+            grads_v,
+            grad_hidden,
+            first_gain,
+            query_weight,
+            key_weight,
+            value_weight,
             sums,
-            jnp.stack([grad_first_gain, grad_first_shift, grad_query_bias, grad_value_bias]),
-        ]
-    )
-    if linked:
-        sums_late, packed, other_in = reduce_all(grads_late, LATE, packed, grad_in[local_len:], 1)
+            LATE,
+            1,
+        )
         grad_inputs = in_order(grad_in[:local_len], other_in)
     else:
+
+        def join(partial):
+            far = lax.ppermute(partial[tokens_here:], "seq", beside)
+            return (partial[:tokens_here].astype(jnp.float32) + far.astype(jnp.float32)).astype(low)
 
         def reduced(partial):
             piece = lax.psum_scatter(partial, ("dp", "seq"), scatter_dimension=0, tiled=True)
             return lax.all_gather(piece, "seq", axis=0, tiled=True).astype(jnp.float32)
 
+        grad_q, grad_k, grad_v = attend_back(*back_args)
+        grads = (grad_q, join(grad_k), join(grad_v))
+        weights = (query_weight, key_weight, value_weight)
+        _, norm_one_back = jax.vjp(
+            norm_apply, both_in.astype(jnp.float32), first_gain, first_shift
+        )
+        grad_in_norm, grad_first_gain, grad_first_shift = norm_one_back(
+            sum(dot(grad, weight, NT) for grad, weight in zip(grads, weights))
+        )
+        late = [jnp.sum(item, axis=0, dtype=jnp.float32) for item in (grads[0], grads[2])]
+        packed = jnp.concatenate([sums, jnp.stack([grad_first_gain, grad_first_shift, *late])])
+        packed = lax.psum(packed, ("dp", "seq"))
         result = give_back(stream)
-        grad_inputs = give_back(grad_in)
+        grad_inputs = give_back((grad_hidden + grad_in_norm).astype(low))
         sums_early = [reduced(item) for item in grads_early]
-        sums_late = [reduced(item) for item in grads_late]
-        packed = lax.psum(packed, ("dp", "seq"))
+        sums_late = [reduced(dot(normed_one_low, grad, TN).astype(low)) for grad in grads]
     summed_outer, summed_inner, summed_output = sums_early
     summed_query, summed_key, summed_value = sums_late
     inner_rows = inner_weight.shape[1] // width

time: 320 us -> 316 us (0.988)
  matrix products: 14.2 us -> 0 us
  Pallas kernels: 260 us -> 272 us
  other arithmetic: 15.5 us -> 7.99 us
  local copies, waits for them, and re-layouts: 18.2 us -> 23.3 us
    dot_general x6 -> x0, matrix products: 14.2 us -> none  [the longest x3 6.84 us: dot(): lax.dot_general(left, right, (dims, ((), ())), preferred_element_type=jnp...]
    pallas_call x1, Pallas kernels: 38 us -> 50.7 us  [leave(): pl.pallas_call(functools.partial(leave_body, orders), out_shape=outs, in_...]
    unnamed x68 -> x52, local copies, waits for them, and re-layouts: 9.19 us -> 7.83 us
where the time goes in v2:
time: 316 us; the launch traced here: 311 us
  Pallas kernels  272 us (86%)
  local copies, waits for them, and re-layouts  23.3 us (7%)
  other arithmetic  7.99 us (3%)
  between operations  7.51 us (2%)
    pallas_call x1, Pallas kernels, attend_back_reduce(): pl.pallas_call(functools.partial(attend_back_reduce_body, len(arrays), or...  95.8 us
    pallas_call x1, Pallas kernels, feed(): pl.pallas_call(feed_body, grid_spec=pltpu.PrefetchScalarGridSpec(num_scal...  51 us
    pallas_call x1, Pallas kernels, leave(): pl.pallas_call(functools.partial(leave_body, orders), out_shape=outs, in_...  50.7 us
    pallas_call x1, Pallas kernels, attend(): pl.pallas_call(attend_body, grid_spec=pltpu.PrefetchScalarGridSpec(num_sc...  46.9 us
    pallas_call x1, Pallas kernels, enter(): pl.pallas_call(enter_body, out_shape=[made(2), made(2), made(2), made(4),...  27.8 us
    unnamed x52, local copies, waits for them, and re-layouts  7.83 us

profile of v2, /device:TPU:0, one launch (start us, length us, event | category | flops | bytes accessed | tf_op | source)
XLA Modules:
  0.0 310.9 jit_solution(9891872280206502931)
XLA Ops:
  0.7 0.0 copy-start
  0.7 0.8 broadcast_in_dim.28.gain_ref
  1.5 0.7 broadcast_in_dim.29.shift_ref
  2.2 0.7 broadcast_in_dim.30.q_bias_ref
  2.9 0.7 broadcast_in_dim.31.v_bias_ref
  3.5 1.3 broadcast_in_dim.34.out_bias_ref
  4.8 1.3 broadcast_in_dim.32.gain_ref
  6.1 1.3 broadcast_in_dim.33.shift_ref
  7.3 1.3 broadcast_in_dim.35.outer_bias_ref
  8.6 2.1 dynamic-slice_bitcast_fusion.cot_ref
  10.7 0.0 copy-done
  10.7 1.3 copy-done.1
  12.0 1.3 copy-done.2
  13.2 27.8 %enter.1 = (bf16[1024,768]{1,0:T(8,128)(2,1)S(1)}, bf16[1024,768]{1,0:T(8,128)(2,1)}, bf16[1024,768]{1,0:T(8,128)(2,1)}, bf16[2048,768]{1,0:T(8,128)(2,1)}, bf16[2048,768]{1,0:T(8,128)(2,1)}) custom-call(bf16[2,512,768]{2,1,0:T(8,128)(2,1)} %in_ref.1, f32[1,768]{1,0:T(1,128)S(1)} %broadcast_in_dim.28.gain_ref, f32[1,768]{1,0:T(1,128)S(1)} %broadcast_in_dim.29.shift_ref, ...), custom_call_target="tpu_custom_call" | custom-call | tf_op jit(solution)/shard_map/enter/pallas_call | solution.py:460
  41.1 0.0 copy-start.5
  41.1 1.1 copy-done.5
  42.2 0.0 copy-done.3
  42.2 1.4 copy-done.6
  43.6 46.9 %attend.1 = (bf16[1024,768]{1,0:T(8,128)(2,1)S(1)}, f32[6,2,1024]{2,1,0:T(2,128)S(1)}, bf16[512,768]{1,0:T(8,128)(2,1)S(1)}) custom-call(s32[2]{0:T(128)S(1)} %copy-done.7, bf16[1024,768]{1,0:T(8,128)(2,1)S(1)} %copy-done.6, bf16[2048,768]{1,0:T(8,128)(2,1)} %get-tuple-element.58.k_ref.refs_2_, bf16[2048,768]{1,0:T(8,128)(2,1)} %get-tuple-element.59.v_ref.refs_3_, ...), custom_call_target="tpu_custom_call" | custom-call | flops 25769803776 | bytes 8388608 | tf_op jit(solution)/shard_map/attend/pallas_call | solution.py:104
  90.5 0.0 copy-start.8
  90.5 1.1 copy-done.8
  91.7 0.9 copy-done.9
  92.6 0.6 copy-done.10
  93.2 51.0 %feed.1 = (bf16[1024,768]{1,0:T(8,128)(2,1)}, bf16[1024,768]{1,0:T(8,128)(2,1)}, f32[1024,768]{1,0:T(8,128)}, f32[12,768]{1,0:T(8,128)}, bf16[3072,768]{1,0:T(8,...) custom-call(s32[2]{0:T(128)} %refs_0_.1, bf16[1024,768]{1,0:T(8,128)(2,1)} %copy-done.5, ...), custom_call_target="tpu_custom_call" | custom-call | flops 32614907904 | bytes 33554432 | tf_op jit(solution)/shard_map/feed/pallas_call | solution.py:962
  144.2 2.4 slice_bitcast_fusion.1
  146.5 95.8 %attend_back_reduce.1 = (bf16[1024,768]{1,0:T(8,128)(2,1)}, bf16[1024,768]{1,0:T(8,128)(2,1)}, bf16[1024,768]{1,0:T(8,128)(2,1)}, bf16[2,192,384]{2,1,0:T(8,128)...) custom-call(s32[2]{0:T(128)} %refs_0_.1, ...), custom_call_target="tpu_custom_call" | custom-call | flops 64424509440 | bytes 33554432 | tf_op jit(solution)/shard_map/attend_back_reduce/pallas_call | solution.py:730
  242.3 50.7 %leave.1 = (bf16[2,48,384]{2,1,0:T(8,128)(2,1)}, bf16[2,48,384]{2,1,0:T(8,128)(2,1)}, bf16[2,48,384]{2,1,0:T(8,128)(2,1)}, bf16[2,48,384]{2,1,0:T(8,128)(2,1)}, ...) custom-call(bf16[1024,768]{1,0:T(8,128)(2,1)} %copy-done.5, ...), custom_call_target="tpu_custom_call" | custom-call | flops 17179869184 | bytes 16777216 | tf_op jit(solution)/shard_map/leave/pallas_call | solution.py:621
  293.0 1.3 slice.74
  295.0 1.2 slice_bitcast_fusion
  296.2 0.0 copy-done.11
  296.2 0.0 copy-done.12
  296.2 0.0 copy-start.25
  296.2 0.0 copy-start.17
  296.2 0.0 copy-start.18
  296.2 0.0 copy-start.23
  296.2 0.0 copy-start.24
  296.2 1.9 maximum_select_fusion
  298.2 0.7 slice_reduce_fusion
  301.0 0.6 reshape.91
  301.7 0.7 maximum_convert_fusion.5
  302.5 0.7 maximum_convert_fusion.2
  303.2 0.0 copy-done.20
  303.2 0.7 maximum_convert_fusion.4
  304.0 0.7 maximum_convert_fusion.3
  304.7 0.0 copy-done.15
  304.8 0.1 broadcast_select_fusion.1
  304.9 1.1 maximum_convert_fusion
  306.0 1.1 maximum_convert_fusion.1
  (35 shorter events, 0.2 us)
Async XLA Ops:
  0.7 10.0 %copy-start = (bf16[768,768]{1,0:T(8,128)(2,1)S(1)}, bf16[768,768]{1,0:T(8,128)(2,1)}, u32[]{:S(2)}) copy-start(bf16[768,768]{1,0:T(8,128)(2,1)} %wq_ref.3) | copy-start | bytes 3538948
  1.5 39.6 %copy-start.4 = (f32[1,768]{1,0:T(1,128)}, f32[1,768]{1,0:T(1,128)S(1)}, u32[]{:S(2)}) copy-start(f32[1,768]{1,0:T(1,128)S(1)} %broadcast_in_dim.28.gain_ref) | copy-start | bytes 9220
  10.7 1.3 copy-start.1
  12.0 1.3 copy-start.2
  13.2 29.0 %copy-start.3 = (bf16[2,512,768]{2,1,0:T(8,128)(2,1)S(1)}, bf16[2,512,768]{2,1,0:T(8,128)(2,1)}, u32[]{:S(2)}) copy-start(bf16[2,512,768]{2,1,0:T(8,128)(2,1)} %cot_ref.1) | copy-start | bytes 4718596
  13.2 29.0 %copy-start.7 = (s32[2]{0:T(128)S(1)}, s32[2]{0:T(128)}, u32[]{:S(2)}) copy-start(s32[2]{0:T(128)} %refs_0_.1) | copy-start | bytes 28
  41.1 1.1 copy-start.5
  42.2 1.4 copy-start.6
  90.5 1.1 copy-start.8
  91.7 0.9 copy-start.9
  92.6 0.6 copy-start.10
  293.0 3.2 %copy-start.11 = (bf16[512,768]{1,0:T(8,128)(2,1)S(1)}, bf16[512,768]{1,0:T(8,128)(2,1)}, u32[]{:S(2)}) copy-start(bf16[512,768]{1,0:T(8,128)(2,1)} %get-tuple-element.68) | copy-start | bytes 2359300
  293.0 3.2 %copy-start.12 = (bf16[512,768]{1,0:T(8,128)(2,1)S(1)}, bf16[512,768]{1,0:T(8,128)(2,1)}, u32[]{:S(2)}) copy-start(bf16[512,768]{1,0:T(8,128)(2,1)} %get-tuple-element.78) | copy-start | bytes 2359300
  296.2 2.0 copy-start.25
  296.2 5.5 %copy-start.17 = (bf16[2,48,384]{2,1,0:T(8,128)(2,1)S(1)}, bf16[2,48,384]{2,1,0:T(8,128)(2,1)}, u32[]{:S(2)}) copy-start(bf16[2,48,384]{2,1,0:T(8,128)(2,1)} %get-tuple-element.86) | copy-start | bytes 221188
  296.2 5.5 %copy-start.18 = (bf16[2,48,384]{2,1,0:T(8,128)(2,1)S(1)}, bf16[2,48,384]{2,1,0:T(8,128)(2,1)}, u32[]{:S(2)}) copy-start(bf16[2,48,384]{2,1,0:T(8,128)(2,1)} %get-tuple-element.87) | copy-start | bytes 221188
  296.2 5.5 %copy-start.23 = (bf16[2,48,384]{2,1,0:T(8,128)(2,1)S(1)}, bf16[2,48,384]{2,1,0:T(8,128)(2,1)}, u32[]{:S(2)}) copy-start(bf16[2,48,384]{2,1,0:T(8,128)(2,1)} %get-tuple-element.80) | copy-start | bytes 221188
  296.2 5.4 %copy-start.24 = (bf16[2,48,384]{2,1,0:T(8,128)(2,1)S(1)}, bf16[2,48,384]{2,1,0:T(8,128)(2,1)}, u32[]{:S(2)}) copy-start(bf16[2,48,384]{2,1,0:T(8,128)(2,1)} %get-tuple-element.81) | copy-start | bytes 221188
  298.2 5.0 %copy-start.19 = (bf16[2,48,384]{2,1,0:T(8,128)(2,1)S(1)}, bf16[2,48,384]{2,1,0:T(8,128)(2,1)}, u32[]{:S(2)}) copy-start(bf16[2,48,384]{2,1,0:T(8,128)(2,1)} %get-tuple-element.82) | copy-start | bytes 221188
  298.2 5.0 %copy-start.20 = (bf16[2,48,384]{2,1,0:T(8,128)(2,1)S(1)}, bf16[2,48,384]{2,1,0:T(8,128)(2,1)}, u32[]{:S(2)}) copy-start(bf16[2,48,384]{2,1,0:T(8,128)(2,1)} %get-tuple-element.83) | copy-start | bytes 221188
  298.2 5.0 %copy-start.21 = (bf16[2,48,384]{2,1,0:T(8,128)(2,1)S(1)}, bf16[2,48,384]{2,1,0:T(8,128)(2,1)}, u32[]{:S(2)}) copy-start(bf16[2,48,384]{2,1,0:T(8,128)(2,1)} %get-tuple-element.84) | copy-start | bytes 221188
  298.2 5.0 %copy-start.22 = (bf16[2,48,384]{2,1,0:T(8,128)(2,1)S(1)}, bf16[2,48,384]{2,1,0:T(8,128)(2,1)}, u32[]{:S(2)}) copy-start(bf16[2,48,384]{2,1,0:T(8,128)(2,1)} %get-tuple-element.85) | copy-start | bytes 221188
  298.2 6.5 %copy-start.15 = (bf16[2,48,1536]{2,1,0:T(8,128)(2,1)S(1)}, bf16[2,48,1536]{2,1,0:T(8,128)(2,1)}, u32[]{:S(2)}) copy-start(bf16[2,48,1536]{2,1,0:T(8,128)(2,1)} %get-tuple-element.88) | copy-start | bytes 884740
  298.2 6.5 %copy-start.16 = (bf16[2,48,1536]{2,1,0:T(8,128)(2,1)S(1)}, bf16[2,48,1536]{2,1,0:T(8,128)(2,1)}, u32[]{:S(2)}) copy-start(bf16[2,48,1536]{2,1,0:T(8,128)(2,1)} %get-tuple-element.89) | copy-start | bytes 884740
  302.4 2.3 copy-start.13
  302.5 2.3 copy-start.14
